TPU v7x, 256 devices: a whole 4x4x8 slice. The times are simulated.
256 devices in a mesh: tile: 128 (over x, z, y), frame: 2 (over core).
Axes of the slice: x: 4, y: 4, z: 8, core: 2. Of those that a mesh axis runs over, the one named last changes fastest.
Arguments:
- movie_block: bfloat16 [128, 8192, 512], P('frame', 'tile'), may hold values from 0 to 0.19921875
- patches: bfloat16 [4096, 64, 64], P('tile'), may hold values from 0.0049743652 to 0.049804688
- patch_rows: int32 [4096], P('tile'), may hold values from -32 to 31
- patch_cols: int32 [4096], P('tile'), may hold values from 0 to 63
- neuron_live: int32 [4096], P('tile'), may hold values from 0 to 1
- neuron_colour: int32 [4096], replicated, may hold values from 0 to 15, as said below
- traces: float32 [4096, 128], P('tile', 'frame'), may hold values from 0.2 to 2
Outputs:
- new_traces: float32 [4096, 128], P('tile', 'frame')
- new_patches: bfloat16 [4096, 64, 64], P('tile')
Inputs may be any that keep to these rules, and one draw needn't show every extreme that they name: `neuron_colour`: slots of one colour never share a pixel: within one tile and column bin every slot has its own colour, and the colours of a bin in a tile and in an adjacent tile are disjoint.
All inputs are finite; a program needn't handle non-finite values.
Results may differ from a plain program's by a relative error of at most 0.005.
Values may be sent and summed in bfloat16 or wider, within the bound.
No kernel may reach another device: no remote copies, remote signals or barrier semaphores. Data moves between devices by JAX's collectives and lax.ppermute only.
A program may use at most 64 MiB of HBM per device.

v0:
```python
import jax
import jax.numpy as jnp
from jax import lax
from jax.sharding import PartitionSpec as P

floor_share = 0.25
exact = lax.Precision.HIGHEST


def extended_2(value, sides, width):
    for axis, dim in sides:
        size, length = (lax.axis_size(axis), value.shape[dim])
        up = [(i, (i + 1) % size) for i in range(size - 1)]
        down = [(j, i) for i, j in up]
        last = lax.slice_in_dim(value, length - width, length, axis=dim)
        initial = lax.slice_in_dim(value, 0, width, axis=dim)
        before = lax.ppermute(last, axis, up)
        after = lax.ppermute(initial, axis, down)
        value = jnp.concatenate([before, value, after], axis=dim)
    return value


def placement_tables(rows_offset, cols_offset, slab_edge, patch_side):
    slab_lines = jnp.arange(slab_edge, dtype=jnp.int32)
    patch_lines = jnp.arange(patch_side, dtype=jnp.int32)
    half_side = patch_side // 2
    row_pick = (
        slab_lines[None, :, None]
        == (half_side + rows_offset)[:, None, None] + patch_lines[None, None, :]
    )
    col_pick = patch_lines[None, :, None] + cols_offset[:, None, None] == slab_lines[None, None, :]
    return (row_pick, col_pick)


def on_device(movie_block, patches, patch_rows, patch_cols, neuron_live, neuron_colour, traces):
    frames_dev, patch_side, image_width = movie_block.shape
    slot_count = patches.shape[0]
    half_side = patch_side // 2
    slab_edge = 2 * patch_side
    bin_count = image_width // slab_edge
    layers = slot_count // bin_count
    colours = 2 * layers
    tile_index = lax.axis_index("tile")
    tile_count = lax.axis_size("tile")
    all_frames = frames_dev * lax.axis_size("frame")

    def by_bins(values):
        return values.reshape((bin_count, layers) + values.shape[1:])

    row_pick, col_pick = placement_tables(patch_rows, patch_cols, slab_edge, patch_side)
    slab_lines = jnp.arange(slab_edge, dtype=jnp.int32)
    image_row = patch_side * tile_index - half_side + slab_lines
    inside = (image_row >= 0) & (image_row < patch_side * tile_count)
    row_ok = jnp.any(row_pick, axis=2) & inside[None, :] & (neuron_live[:, None] > 0)
    col_ok = jnp.any(col_pick, axis=1)
    support = row_ok[:, :, None] & col_ok[:, None, :]
    placed = jnp.einsum(
        "nei,nij->nej", row_pick.astype(jnp.bfloat16), patches, preferred_element_type=jnp.float32
    ).astype(jnp.bfloat16)
    spread = jnp.einsum(
        "nej,njc->nec", placed, col_pick.astype(jnp.bfloat16), preferred_element_type=jnp.float32
    )
    slabs = jnp.where(support, spread, 0.0).astype(jnp.bfloat16)
    rimmed = extended_2(slabs, (("tile", 1),), patch_side)
    below_prev = by_bins(rimmed[:, :patch_side])
    above_next = by_bins(rimmed[:, patch_side + slab_edge :])
    slab_grid = by_bins(slabs)
    support_grid = by_bins(support)
    gram_own = jnp.einsum(
        "bnec,bmec->bnm", slab_grid, slab_grid, preferred_element_type=jnp.float32
    )
    gram_prev = jnp.einsum(
        "bnec,bmec->bnm",
        slab_grid[:, :, :patch_side],
        below_prev,
        preferred_element_type=jnp.float32,
    )
    gram_next = jnp.einsum(
        "bnec,bmec->bnm",
        slab_grid[:, :, patch_side:],
        above_next,
        preferred_element_type=jnp.float32,
    )
    extended = extended_2(movie_block, (("tile", 1),), half_side)
    extended_bins = extended.reshape(frames_dev, slab_edge, bin_count, slab_edge)
    drive = jnp.einsum(
        "bnec,febc->bnf", slab_grid, extended_bins, preferred_element_type=jnp.float32
    )

    def neighbour_traces(current):
        rimmed_now = extended_2(current, (("tile", 0),), slot_count)
        return (by_bins(rimmed_now[:slot_count]), by_bins(rimmed_now[2 * slot_count :]))

    own_colour = lax.dynamic_slice_in_dim(neuron_colour, tile_index * slot_count, slot_count)
    colour_grid = by_bins(own_colour)
    alive_mask = neuron_live.astype(jnp.float32)
    denominator = jnp.diagonal(gram_own, axis1=1, axis2=2) + (1.0 - by_bins(alive_mask))

    def temporal_step(colour_now, current):
        before, after = neighbour_traces(current)
        grid_now = by_bins(current)
        coupled = jnp.einsum("bnm,bmf->bnf", gram_own, grid_now, precision=exact)
        coupled = coupled + jnp.einsum("bnm,bmf->bnf", gram_prev, before, precision=exact)
        coupled = coupled + jnp.einsum("bnm,bmf->bnf", gram_next, after, precision=exact)
        proposal = jnp.maximum(grid_now + (drive - coupled) / denominator[:, :, None], 0.0)
        chosen = (colour_grid == colour_now)[:, :, None]
        return jnp.where(chosen, proposal, grid_now).reshape(slot_count, frames_dev)

    start = traces * alive_mask[:, None]
    settled = lax.fori_loop(0, colours, temporal_step, start)
    before, after = neighbour_traces(settled)
    settled_grid = by_bins(settled)
    rounded = settled_grid.astype(jnp.bfloat16)
    cross_own = jnp.einsum("bnf,bmf->bnm", settled_grid, settled_grid, precision=exact)
    cross_prev = jnp.einsum("bnf,bmf->bnm", settled_grid, before, precision=exact)
    cross_next = jnp.einsum("bnf,bmf->bnm", settled_grid, after, precision=exact)
    field = jnp.einsum("febc,bnf->bnec", extended_bins, rounded, preferred_element_type=jnp.float32)
    field, cross_own, cross_prev, cross_next = lax.psum(
        (field, cross_own, cross_prev, cross_next), "frame"
    )
    spatial_den = jnp.maximum(jnp.diagonal(cross_own, axis1=1, axis2=2), floor_share * all_frames)

    def coupling(state, upper, lower):
        state_float = state.astype(jnp.float32)
        top = jnp.einsum(
            "bnm,bmec->bnec", cross_own, state_float[:, :, :patch_side], precision=exact
        )
        top = top + jnp.einsum(
            "bnm,bmec->bnec", cross_prev, upper.astype(jnp.float32), precision=exact
        )
        bottom = jnp.einsum(
            "bnm,bmec->bnec", cross_own, state_float[:, :, patch_side:], precision=exact
        )
        bottom = bottom + jnp.einsum(
            "bnm,bmec->bnec", cross_next, lower.astype(jnp.float32), precision=exact
        )
        return (state_float, jnp.concatenate([top, bottom], axis=2))

    def renew(state_float, mixed, colour_now):
        proposal = jnp.maximum(state_float + (field - mixed) / spatial_den[:, :, None, None], 0.0)
        chosen = (colour_grid == colour_now)[:, :, None, None]
        return jnp.where(chosen, jnp.where(support_grid, proposal, 0.0), state_float).astype(
            jnp.bfloat16
        )

    def spatial_step(colour_now, state):
        rimmed_now = extended_2(state, (("tile", 2),), patch_side)
        state_float, mixed = coupling(
            state, rimmed_now[:, :, :patch_side], rimmed_now[:, :, patch_side + slab_edge :]
        )
        return renew(state_float, mixed, colour_now)

    final = lax.fori_loop(0, colours, spatial_step, slab_grid)
    share_slots = bin_count * layers
    final_flat = final.reshape(share_slots, slab_edge, slab_edge)
    row_share = by_bins(row_pick).reshape(share_slots, slab_edge, patch_side)
    col_share = by_bins(col_pick).reshape(share_slots, patch_side, slab_edge)
    lifted = jnp.einsum(
        "nei,nec->nic",
        row_share.astype(jnp.bfloat16),
        final_flat,
        preferred_element_type=jnp.float32,
    ).astype(jnp.bfloat16)
    new_patches = jnp.einsum(
        "nic,njc->nij", lifted, col_share.astype(jnp.bfloat16), preferred_element_type=jnp.float32
    ).astype(jnp.bfloat16)
    return (settled, new_patches)


def solution(mesh):
    placed = (
        P("frame", "tile", None),
        P("tile", None, None),
        P("tile"),
        P("tile"),
        P("tile"),
        P(),
        P("tile", "frame"),
    )
    return jax.shard_map(
        on_device,
        mesh=mesh,
        in_specs=placed,
        out_specs=(P("tile", "frame"), P("tile", None, None)),
        check_vma=False,
    )
```

profile of v0, /device:TPU:6, one launch (start us, length us, event | category | flops | bytes accessed | tf_op | source)
XLA Modules:
  0.0 715.0 jit_solution(2921657273036980261)
XLA Ops:
  7.3 4.8 fusion.49
  15.6 8.9 %collective-permute-start.7 = (bf16[64,32,512]{2,1,0:T(8,128)(2,1)}, bf16[64,32,512]{2,1,0:T(8,128)(2,1)}, u32[]{:S(2)}, u32[]{:S(2)}) collective-permute-start(bf16[64,32,512]{2,1,0:T(8,128)(2,1)} %get-tuple-element.417), channel_id=1, source_target_pairs={{2,0},{4,2},{6,4},{8,6},{10,8},{12,10},{14,12},{16,14},{18,16},{20... | collective-permute-start | bytes 6291464 | tf_op jit(solution)/shard_map/ppermute | solution.py:18
  37.6 43.3 %collective-permute-done.5 = bf16[32,64,128]{2,1,0:T(8,128)(2,1)} collective-permute-done((bf16[32,64,128]{2,1,0:T(8,128)(2,1)}, bf16[32,64,128]{2,1,0:T(8,128)(2,1)}, u32[]{:S(2)}, u32[]{:S(2)}) %collective-permute-start.5) | collective-permute-done | bytes 524320 | tf_op jit(solution)/shard_map/ppermute | solution.py:18
  84.7 6.1 pad_maximum_fusion
  90.8 12.0 %copy.48 = bf16[64,128,512]{1,0,2:T(8,128)(2,1)} copy(bf16[64,128,512]{2,1,0:T(8,128)(2,1)} %pad_maximum_fusion) | data formatting | bytes 16777216 | tf_op jit(solution)/shard_map/concatenate | solution.py:19
  102.8 5.6 convolution_bitcast_fusion.2
  108.4 13.5 %copy.53 = bf16[64,128,4,128]{3,0,1,2:T(8,128)(2,1)} copy(bf16[64,128,4,128]{1,0,3,2:T(8,128)(2,1)} %bitcast.120) | data formatting | bytes 16777216 | tf_op jit(solution)/shard_map/reshape | solution.py:85
  121.9 191.6 %while.27 = (s32[]{:T(128)}, f32[32,64]{1,0:T(8,128)S(1)}, s32[4,8]{1,0:T(4,128)S(1)}, f32[4,8,8]{2,1,0:T(8,128)S(1)}, f32[4,8,8]{2,1,0:T(8,128)S(1)}, /*index=5...) while((s32[]{:T(128)}, f32[32,64]{1,0:T(8,128)S(1)}, ...), condition=%wide.region_3.4_spmd, body=%wide.region_2.3_spmd.sunk | while | flops 604194 | bytes 151025 | solution.py:110
  123.8 8.6 %collective-permute-start.1 = (f32[32,64]{1,0:T(8,128)S(1)}, f32[32,64]{1,0:T(8,128)S(1)}, u32[]{:S(2)}, u32[]{:S(2)}) collective-permute-start(f32[32,64]{1,0:T(8,128)S(1)} %get-tuple-element.546), channel_id=1, source_target_pairs={{2,0},{4,2},{6,4},{8,6},{10,8},{12,10},{14,12},{16,14},{18,16},{20... | collective-permute-start | bytes 24584 | tf_op jit(solution)/shard_map/while/body/eval_jaxpr/ppermute | solution.py:18
  136.0 8.4 %collective-permute-start.1 = (f32[32,64]{1,0:T(8,128)S(1)}, f32[32,64]{1,0:T(8,128)S(1)}, u32[]{:S(2)}, u32[]{:S(2)}) collective-permute-start(f32[32,64]{1,0:T(8,128)S(1)} %get-tuple-element.546), channel_id=1, source_target_pairs={{2,0},{4,2},{6,4},{8,6},{10,8},{12,10},{14,12},{16,14},{18,16},{20... | collective-permute-start | bytes 24584 | tf_op jit(solution)/shard_map/while/body/eval_jaxpr/ppermute | solution.py:18
  148.0 8.4 %collective-permute-start.1 = (f32[32,64]{1,0:T(8,128)S(1)}, f32[32,64]{1,0:T(8,128)S(1)}, u32[]{:S(2)}, u32[]{:S(2)}) collective-permute-start(f32[32,64]{1,0:T(8,128)S(1)} %get-tuple-element.546), channel_id=1, source_target_pairs={{2,0},{4,2},{6,4},{8,6},{10,8},{12,10},{14,12},{16,14},{18,16},{20... | collective-permute-start | bytes 24584 | tf_op jit(solution)/shard_map/while/body/eval_jaxpr/ppermute | solution.py:18
  159.9 8.4 %collective-permute-start.1 = (f32[32,64]{1,0:T(8,128)S(1)}, f32[32,64]{1,0:T(8,128)S(1)}, u32[]{:S(2)}, u32[]{:S(2)}) collective-permute-start(f32[32,64]{1,0:T(8,128)S(1)} %get-tuple-element.546), channel_id=1, source_target_pairs={{2,0},{4,2},{6,4},{8,6},{10,8},{12,10},{14,12},{16,14},{18,16},{20... | collective-permute-start | bytes 24584 | tf_op jit(solution)/shard_map/while/body/eval_jaxpr/ppermute | solution.py:18
  171.9 8.4 %collective-permute-start.1 = (f32[32,64]{1,0:T(8,128)S(1)}, f32[32,64]{1,0:T(8,128)S(1)}, u32[]{:S(2)}, u32[]{:S(2)}) collective-permute-start(f32[32,64]{1,0:T(8,128)S(1)} %get-tuple-element.546), channel_id=1, source_target_pairs={{2,0},{4,2},{6,4},{8,6},{10,8},{12,10},{14,12},{16,14},{18,16},{20... | collective-permute-start | bytes 24584 | tf_op jit(solution)/shard_map/while/body/eval_jaxpr/ppermute | solution.py:18
  183.8 8.4 %collective-permute-start.1 = (f32[32,64]{1,0:T(8,128)S(1)}, f32[32,64]{1,0:T(8,128)S(1)}, u32[]{:S(2)}, u32[]{:S(2)}) collective-permute-start(f32[32,64]{1,0:T(8,128)S(1)} %get-tuple-element.546), channel_id=1, source_target_pairs={{2,0},{4,2},{6,4},{8,6},{10,8},{12,10},{14,12},{16,14},{18,16},{20... | collective-permute-start | bytes 24584 | tf_op jit(solution)/shard_map/while/body/eval_jaxpr/ppermute | solution.py:18
  195.8 8.4 %collective-permute-start.1 = (f32[32,64]{1,0:T(8,128)S(1)}, f32[32,64]{1,0:T(8,128)S(1)}, u32[]{:S(2)}, u32[]{:S(2)}) collective-permute-start(f32[32,64]{1,0:T(8,128)S(1)} %get-tuple-element.546), channel_id=1, source_target_pairs={{2,0},{4,2},{6,4},{8,6},{10,8},{12,10},{14,12},{16,14},{18,16},{20... | collective-permute-start | bytes 24584 | tf_op jit(solution)/shard_map/while/body/eval_jaxpr/ppermute | solution.py:18
  207.8 8.4 %collective-permute-start.1 = (f32[32,64]{1,0:T(8,128)S(1)}, f32[32,64]{1,0:T(8,128)S(1)}, u32[]{:S(2)}, u32[]{:S(2)}) collective-permute-start(f32[32,64]{1,0:T(8,128)S(1)} %get-tuple-element.546), channel_id=1, source_target_pairs={{2,0},{4,2},{6,4},{8,6},{10,8},{12,10},{14,12},{16,14},{18,16},{20... | collective-permute-start | bytes 24584 | tf_op jit(solution)/shard_map/while/body/eval_jaxpr/ppermute | solution.py:18
  219.7 8.4 %collective-permute-start.1 = (f32[32,64]{1,0:T(8,128)S(1)}, f32[32,64]{1,0:T(8,128)S(1)}, u32[]{:S(2)}, u32[]{:S(2)}) collective-permute-start(f32[32,64]{1,0:T(8,128)S(1)} %get-tuple-element.546), channel_id=1, source_target_pairs={{2,0},{4,2},{6,4},{8,6},{10,8},{12,10},{14,12},{16,14},{18,16},{20... | collective-permute-start | bytes 24584 | tf_op jit(solution)/shard_map/while/body/eval_jaxpr/ppermute | solution.py:18
  231.7 8.4 %collective-permute-start.1 = (f32[32,64]{1,0:T(8,128)S(1)}, f32[32,64]{1,0:T(8,128)S(1)}, u32[]{:S(2)}, u32[]{:S(2)}) collective-permute-start(f32[32,64]{1,0:T(8,128)S(1)} %get-tuple-element.546), channel_id=1, source_target_pairs={{2,0},{4,2},{6,4},{8,6},{10,8},{12,10},{14,12},{16,14},{18,16},{20... | collective-permute-start | bytes 24584 | tf_op jit(solution)/shard_map/while/body/eval_jaxpr/ppermute | solution.py:18
  243.7 8.4 %collective-permute-start.1 = (f32[32,64]{1,0:T(8,128)S(1)}, f32[32,64]{1,0:T(8,128)S(1)}, u32[]{:S(2)}, u32[]{:S(2)}) collective-permute-start(f32[32,64]{1,0:T(8,128)S(1)} %get-tuple-element.546), channel_id=1, source_target_pairs={{2,0},{4,2},{6,4},{8,6},{10,8},{12,10},{14,12},{16,14},{18,16},{20... | collective-permute-start | bytes 24584 | tf_op jit(solution)/shard_map/while/body/eval_jaxpr/ppermute | solution.py:18
  255.6 8.4 %collective-permute-start.1 = (f32[32,64]{1,0:T(8,128)S(1)}, f32[32,64]{1,0:T(8,128)S(1)}, u32[]{:S(2)}, u32[]{:S(2)}) collective-permute-start(f32[32,64]{1,0:T(8,128)S(1)} %get-tuple-element.546), channel_id=1, source_target_pairs={{2,0},{4,2},{6,4},{8,6},{10,8},{12,10},{14,12},{16,14},{18,16},{20... | collective-permute-start | bytes 24584 | tf_op jit(solution)/shard_map/while/body/eval_jaxpr/ppermute | solution.py:18
  267.6 8.4 %collective-permute-start.1 = (f32[32,64]{1,0:T(8,128)S(1)}, f32[32,64]{1,0:T(8,128)S(1)}, u32[]{:S(2)}, u32[]{:S(2)}) collective-permute-start(f32[32,64]{1,0:T(8,128)S(1)} %get-tuple-element.546), channel_id=1, source_target_pairs={{2,0},{4,2},{6,4},{8,6},{10,8},{12,10},{14,12},{16,14},{18,16},{20... | collective-permute-start | bytes 24584 | tf_op jit(solution)/shard_map/while/body/eval_jaxpr/ppermute | solution.py:18
  279.6 8.4 %collective-permute-start.1 = (f32[32,64]{1,0:T(8,128)S(1)}, f32[32,64]{1,0:T(8,128)S(1)}, u32[]{:S(2)}, u32[]{:S(2)}) collective-permute-start(f32[32,64]{1,0:T(8,128)S(1)} %get-tuple-element.546), channel_id=1, source_target_pairs={{2,0},{4,2},{6,4},{8,6},{10,8},{12,10},{14,12},{16,14},{18,16},{20... | collective-permute-start | bytes 24584 | tf_op jit(solution)/shard_map/while/body/eval_jaxpr/ppermute | solution.py:18
  291.5 8.4 %collective-permute-start.1 = (f32[32,64]{1,0:T(8,128)S(1)}, f32[32,64]{1,0:T(8,128)S(1)}, u32[]{:S(2)}, u32[]{:S(2)}) collective-permute-start(f32[32,64]{1,0:T(8,128)S(1)} %get-tuple-element.546), channel_id=1, source_target_pairs={{2,0},{4,2},{6,4},{8,6},{10,8},{12,10},{14,12},{16,14},{18,16},{20... | collective-permute-start | bytes 24584 | tf_op jit(solution)/shard_map/while/body/eval_jaxpr/ppermute | solution.py:18
  303.5 8.4 %collective-permute-start.1 = (f32[32,64]{1,0:T(8,128)S(1)}, f32[32,64]{1,0:T(8,128)S(1)}, u32[]{:S(2)}, u32[]{:S(2)}) collective-permute-start(f32[32,64]{1,0:T(8,128)S(1)} %get-tuple-element.546), channel_id=1, source_target_pairs={{2,0},{4,2},{6,4},{8,6},{10,8},{12,10},{14,12},{16,14},{18,16},{20... | collective-permute-start | bytes 24584 | tf_op jit(solution)/shard_map/while/body/eval_jaxpr/ppermute | solution.py:18
  313.5 5.9 fusion.44
  320.5 8.4 %collective-permute-start.9 = (f32[32,64]{1,0:T(8,128)S(1)}, f32[32,64]{1,0:T(8,128)S(1)}, u32[]{:S(2)}, u32[]{:S(2)}) collective-permute-start(f32[32,64]{1,0:T(8,128)S(1)} %get-tuple-element.293), channel_id=1, source_target_pairs={{2,0},{4,2},{6,4},{8,6},{10,8},{12,10},{14,12},{16,14},{18,16},{20... | collective-permute-start | bytes 24584 | tf_op jit(solution)/shard_map/ppermute | solution.py:18
  331.2 7.6 %collective-permute-done.8 = f32[32,64]{1,0:T(8,128)S(1)} collective-permute-done((f32[32,64]{1,0:T(8,128)S(1)}, f32[32,64]{1,0:T(8,128)S(1)}, u32[]{:S(2)}, u32[]{:S(2)}) %collective-permute-start.8) | collective-permute-done | bytes 8224 | tf_op jit(solution)/shard_map/ppermute | solution.py:17
  343.5 7.5 %all-reduce.3.cloned.1.call-done = f32[4,8,128,128]{3,1,2,0:T(8,128)} async-done(((f32[4,8,128,128]{3,1,2,0:T(8,128)}), f32[4,8,128,128]{3,1,2,0:T(8,128)}) %all-reduce.3.cloned.1.call-update) | async-done | bytes 2097168 | tf_op jit(solution)/shard_map/psum | solution.py:118
  351.0 355.4 %while.28 = (s32[]{:T(128)}, bf16[4,8,128,128]{3,1,2,0:T(8,128)(2,1)S(1)}, s32[4,8]{1,0:T(4,128)S(1)}, f32[4,8,8]{2,1,0:T(8,128)S(1)}, f32[4,8,8]{2,1,0:T(8,128)...) while((s32[]{:T(128)}, ...), condition=%wide.region_9.10_spmd.clone, body=%wide.region_8.9_spmd.clone.sunk | while | flops 106430496 | bytes 29403684 | solution.py:153
  352.0 7.7 %collective-permute-start.2 = (bf16[4,8,64,128]{3,1,2,0:T(8,128)(2,1)}, bf16[4,8,64,128]{3,1,2,0:T(8,128)(2,1)}, u32[]{:S(2)}, u32[]{:S(2)}) collective-permute-start(bf16[4,8,64,128]{3,1,2,0:T(8,128)(2,1)} %get-tuple-element.534), channel_id=1, source_target_pairs={{2,0},{4,2},{6,4},{8,6},{10,8},{12,10},{14,12},{16,14},{18,16},{20... | collective-permute-start | bytes 1572872 | tf_op jit(solution)/shard_map/while/body/eval_jaxpr/ppermute | solution.py:18
  363.8 7.9 %collective-permute-done.2 = bf16[4,8,64,128]{3,1,2,0:T(8,128)(2,1)} collective-permute-done((bf16[4,8,64,128]{3,1,2,0:T(8,128)(2,1)}, bf16[4,8,64,128]{3,1,2,0:T(8,128)(2,1)}, u32[]{:S(2)}, u32[]{:S(2)}) %collective-permute-start.2) | collective-permute-done | bytes 524320 | tf_op jit(solution)/shard_map/while/body/eval_jaxpr/ppermute | solution.py:18
  373.8 6.1 collective-permute-done.3
  390.9 7.2 %collective-permute-done.2 = bf16[4,8,64,128]{3,1,2,0:T(8,128)(2,1)} collective-permute-done((bf16[4,8,64,128]{3,1,2,0:T(8,128)(2,1)}, bf16[4,8,64,128]{3,1,2,0:T(8,128)(2,1)}, u32[]{:S(2)}, u32[]{:S(2)}) %collective-permute-start.2) | collective-permute-done | bytes 524320 | tf_op jit(solution)/shard_map/while/body/eval_jaxpr/ppermute | solution.py:18
  400.2 4.5 collective-permute-done.3
  415.8 6.4 collective-permute-done.2
  424.3 4.5 collective-permute-done.3
  439.8 5.4 collective-permute-done.2
  447.3 4.5 collective-permute-done.3
  462.8 4.5 collective-permute-done.2
  469.4 4.5 collective-permute-done.3
  490.7 4.5 collective-permute-done.3
  511.7 4.5 collective-permute-done.3
  553.5 4.2 collective-permute-done.3
  574.3 4.2 collective-permute-done.3
  595.1 4.2 collective-permute-done.3
  615.9 4.2 collective-permute-done.3
  636.6 4.2 collective-permute-done.3
  673.0 4.9 collective-permute-done.2
  (364 shorter events, 341.6 us)
Async XLA Ops:
  7.2 343.8 %all-reduce.3.cloned.1.call-start = ((), (), s32[]{:S(2)}) async-start(), calls=%async_computation | async-start | bytes 4194304 | tf_op jit(solution)/shard_map/psum | solution.py:118
  12.1 72.6 %collective-permute-start.6 = (bf16[64,32,512]{2,1,0:T(8,128)(2,1)}, bf16[64,32,512]{2,1,0:T(8,128)(2,1)}, u32[]{:S(2)}, u32[]{:S(2)}) collective-permute-start(bf16[64,32,512]{2,1,0:T(8,128)(2,1)} %get-tuple-element.416), channel_id=1, source_target_pairs={{0,2},{2,4},{4,6},{6,8},{8,10},{10,12},{12,14},{14,16},{16,18},{18... | collective-permute-start | bytes 6291464 | tf_op jit(solution)/shard_map/ppermute | solution.py:17
  15.6 69.1 %collective-permute-start.7 = (bf16[64,32,512]{2,1,0:T(8,128)(2,1)}, bf16[64,32,512]{2,1,0:T(8,128)(2,1)}, u32[]{:S(2)}, u32[]{:S(2)}) collective-permute-start(bf16[64,32,512]{2,1,0:T(8,128)(2,1)} %get-tuple-element.417), channel_id=1, source_target_pairs={{2,0},{4,2},{6,4},{8,6},{10,8},{12,10},{14,12},{16,14},{18,16},{20... | collective-permute-start | bytes 6291464 | tf_op jit(solution)/shard_map/ppermute | solution.py:18
  28.4 52.6 %collective-permute-start.5 = (bf16[32,64,128]{2,1,0:T(8,128)(2,1)}, bf16[32,64,128]{2,1,0:T(8,128)(2,1)}, u32[]{:S(2)}, u32[]{:S(2)}) collective-permute-start(bf16[32,64,128]{2,1,0:T(8,128)(2,1)} %get-tuple-element.418), channel_id=1, source_target_pairs={{2,0},{4,2},{6,4},{8,6},{10,8},{12,10},{14,12},{16,14},{18,16},{20... | collective-permute-start | bytes 1572872 | tf_op jit(solution)/shard_map/ppermute | solution.py:18
  32.3 50.6 %collective-permute-start.4 = (bf16[32,64,128]{2,1,0:T(8,128)(2,1)S(1)}, bf16[32,64,128]{2,1,0:T(8,128)(2,1)}, u32[]{:S(2)}, u32[]{:S(2)}) collective-permute-start(bf16[32,64,128]{2,1,0:T(8,128)(2,1)S(1)} %get-tuple-element.419), channel_id=1, source_target_pairs={{0,2},{2,4},{4,6},{6,8},{8,10},{10,12},{12,14},{14,16},{16,18},{18... | collective-permute-start | bytes 1572872 | tf_op jit(solution)/shard_map/ppermute | solution.py:17
  121.9 10.7 %collective-permute-start = (f32[32,64]{1,0:T(8,128)S(1)}, f32[32,64]{1,0:T(8,128)S(1)}, u32[]{:S(2)}, u32[]{:S(2)}) collective-permute-start(f32[32,64]{1,0:T(8,128)S(1)} %get-tuple-element.546), channel_id=1, source_target_pairs={{0,2},{2,4},{4,6},{6,8},{8,10},{10,12},{12,14},{14,16},{16,18},{18... | collective-permute-start | bytes 24584 | tf_op jit(solution)/shard_map/while/body/eval_jaxpr/ppermute | solution.py:17
  146.0 10.5 %collective-permute-start = (f32[32,64]{1,0:T(8,128)S(1)}, f32[32,64]{1,0:T(8,128)S(1)}, u32[]{:S(2)}, u32[]{:S(2)}) collective-permute-start(f32[32,64]{1,0:T(8,128)S(1)} %get-tuple-element.546), channel_id=1, source_target_pairs={{0,2},{2,4},{4,6},{6,8},{8,10},{10,12},{12,14},{14,16},{16,18},{18... | collective-permute-start | bytes 24584 | tf_op jit(solution)/shard_map/while/body/eval_jaxpr/ppermute | solution.py:17
  181.9 10.5 %collective-permute-start = (f32[32,64]{1,0:T(8,128)S(1)}, f32[32,64]{1,0:T(8,128)S(1)}, u32[]{:S(2)}, u32[]{:S(2)}) collective-permute-start(f32[32,64]{1,0:T(8,128)S(1)} %get-tuple-element.546), channel_id=1, source_target_pairs={{0,2},{2,4},{4,6},{6,8},{8,10},{10,12},{12,14},{14,16},{16,18},{18... | collective-permute-start | bytes 24584 | tf_op jit(solution)/shard_map/while/body/eval_jaxpr/ppermute | solution.py:17
  193.9 10.5 %collective-permute-start = (f32[32,64]{1,0:T(8,128)S(1)}, f32[32,64]{1,0:T(8,128)S(1)}, u32[]{:S(2)}, u32[]{:S(2)}) collective-permute-start(f32[32,64]{1,0:T(8,128)S(1)} %get-tuple-element.546), channel_id=1, source_target_pairs={{0,2},{2,4},{4,6},{6,8},{8,10},{10,12},{12,14},{14,16},{16,18},{18... | collective-permute-start | bytes 24584 | tf_op jit(solution)/shard_map/while/body/eval_jaxpr/ppermute | solution.py:17
  205.8 10.5 %collective-permute-start = (f32[32,64]{1,0:T(8,128)S(1)}, f32[32,64]{1,0:T(8,128)S(1)}, u32[]{:S(2)}, u32[]{:S(2)}) collective-permute-start(f32[32,64]{1,0:T(8,128)S(1)} %get-tuple-element.546), channel_id=1, source_target_pairs={{0,2},{2,4},{4,6},{6,8},{8,10},{10,12},{12,14},{14,16},{16,18},{18... | collective-permute-start | bytes 24584 | tf_op jit(solution)/shard_map/while/body/eval_jaxpr/ppermute | solution.py:17
  217.8 10.5 %collective-permute-start = (f32[32,64]{1,0:T(8,128)S(1)}, f32[32,64]{1,0:T(8,128)S(1)}, u32[]{:S(2)}, u32[]{:S(2)}) collective-permute-start(f32[32,64]{1,0:T(8,128)S(1)} %get-tuple-element.546), channel_id=1, source_target_pairs={{0,2},{2,4},{4,6},{6,8},{8,10},{10,12},{12,14},{14,16},{16,18},{18... | collective-permute-start | bytes 24584 | tf_op jit(solution)/shard_map/while/body/eval_jaxpr/ppermute | solution.py:17
  229.8 10.5 %collective-permute-start = (f32[32,64]{1,0:T(8,128)S(1)}, f32[32,64]{1,0:T(8,128)S(1)}, u32[]{:S(2)}, u32[]{:S(2)}) collective-permute-start(f32[32,64]{1,0:T(8,128)S(1)} %get-tuple-element.546), channel_id=1, source_target_pairs={{0,2},{2,4},{4,6},{6,8},{8,10},{10,12},{12,14},{14,16},{16,18},{18... | collective-permute-start | bytes 24584 | tf_op jit(solution)/shard_map/while/body/eval_jaxpr/ppermute | solution.py:17
  241.7 10.5 %collective-permute-start = (f32[32,64]{1,0:T(8,128)S(1)}, f32[32,64]{1,0:T(8,128)S(1)}, u32[]{:S(2)}, u32[]{:S(2)}) collective-permute-start(f32[32,64]{1,0:T(8,128)S(1)} %get-tuple-element.546), channel_id=1, source_target_pairs={{0,2},{2,4},{4,6},{6,8},{8,10},{10,12},{12,14},{14,16},{16,18},{18... | collective-permute-start | bytes 24584 | tf_op jit(solution)/shard_map/while/body/eval_jaxpr/ppermute | solution.py:17
  253.7 10.5 %collective-permute-start = (f32[32,64]{1,0:T(8,128)S(1)}, f32[32,64]{1,0:T(8,128)S(1)}, u32[]{:S(2)}, u32[]{:S(2)}) collective-permute-start(f32[32,64]{1,0:T(8,128)S(1)} %get-tuple-element.546), channel_id=1, source_target_pairs={{0,2},{2,4},{4,6},{6,8},{8,10},{10,12},{12,14},{14,16},{16,18},{18... | collective-permute-start | bytes 24584 | tf_op jit(solution)/shard_map/while/body/eval_jaxpr/ppermute | solution.py:17
  265.7 10.5 %collective-permute-start = (f32[32,64]{1,0:T(8,128)S(1)}, f32[32,64]{1,0:T(8,128)S(1)}, u32[]{:S(2)}, u32[]{:S(2)}) collective-permute-start(f32[32,64]{1,0:T(8,128)S(1)} %get-tuple-element.546), channel_id=1, source_target_pairs={{0,2},{2,4},{4,6},{6,8},{8,10},{10,12},{12,14},{14,16},{16,18},{18... | collective-permute-start | bytes 24584 | tf_op jit(solution)/shard_map/while/body/eval_jaxpr/ppermute | solution.py:17
  301.5 10.5 %collective-permute-start = (f32[32,64]{1,0:T(8,128)S(1)}, f32[32,64]{1,0:T(8,128)S(1)}, u32[]{:S(2)}, u32[]{:S(2)}) collective-permute-start(f32[32,64]{1,0:T(8,128)S(1)} %get-tuple-element.546), channel_id=1, source_target_pairs={{0,2},{2,4},{4,6},{6,8},{8,10},{10,12},{12,14},{14,16},{16,18},{18... | collective-permute-start | bytes 24584 | tf_op jit(solution)/shard_map/while/body/eval_jaxpr/ppermute | solution.py:17
  352.0 19.6 %collective-permute-start.2 = (bf16[4,8,64,128]{3,1,2,0:T(8,128)(2,1)}, bf16[4,8,64,128]{3,1,2,0:T(8,128)(2,1)}, u32[]{:S(2)}, u32[]{:S(2)}) collective-permute-start(bf16[4,8,64,128]{3,1,2,0:T(8,128)(2,1)} %get-tuple-element.534), channel_id=1, source_target_pairs={{2,0},{4,2},{6,4},{8,6},{10,8},{12,10},{14,12},{16,14},{18,16},{20... | collective-permute-start | bytes 1572872 | tf_op jit(solution)/shard_map/while/body/eval_jaxpr/ppermute | solution.py:18
  359.7 20.2 %collective-permute-start.3 = (bf16[4,8,64,128]{3,1,2,0:T(8,128)(2,1)}, bf16[4,8,64,128]{3,1,2,0:T(8,128)(2,1)S(1)}, u32[]{:S(2)}, u32[]{:S(2)}) collective-permute-start(bf16[4,8,64,128]{3,1,2,0:T(8,128)(2,1)} %get-tuple-element.535), channel_id=1, source_target_pairs={{0,2},{2,4},{4,6},{6,8},{8,10},{10,12},{12,14},{14,16},{16,18},{18... | collective-permute-start | bytes 1572872 | tf_op jit(solution)/shard_map/while/body/eval_jaxpr/ppermute | solution.py:17
  382.9 15.2 %collective-permute-start.2 = (bf16[4,8,64,128]{3,1,2,0:T(8,128)(2,1)}, bf16[4,8,64,128]{3,1,2,0:T(8,128)(2,1)}, u32[]{:S(2)}, u32[]{:S(2)}) collective-permute-start(bf16[4,8,64,128]{3,1,2,0:T(8,128)(2,1)} %get-tuple-element.534), channel_id=1, source_target_pairs={{2,0},{4,2},{6,4},{8,6},{10,8},{12,10},{14,12},{16,14},{18,16},{20... | collective-permute-start | bytes 1572872 | tf_op jit(solution)/shard_map/while/body/eval_jaxpr/ppermute | solution.py:18
  385.4 19.4 %collective-permute-start.3 = (bf16[4,8,64,128]{3,1,2,0:T(8,128)(2,1)}, bf16[4,8,64,128]{3,1,2,0:T(8,128)(2,1)S(1)}, u32[]{:S(2)}, u32[]{:S(2)}) collective-permute-start(bf16[4,8,64,128]{3,1,2,0:T(8,128)(2,1)} %get-tuple-element.535), channel_id=1, source_target_pairs={{0,2},{2,4},{4,6},{6,8},{8,10},{10,12},{12,14},{14,16},{16,18},{18... | collective-permute-start | bytes 1572872 | tf_op jit(solution)/shard_map/while/body/eval_jaxpr/ppermute | solution.py:17
  407.8 14.3 %collective-permute-start.2 = (bf16[4,8,64,128]{3,1,2,0:T(8,128)(2,1)}, bf16[4,8,64,128]{3,1,2,0:T(8,128)(2,1)}, u32[]{:S(2)}, u32[]{:S(2)}) collective-permute-start(bf16[4,8,64,128]{3,1,2,0:T(8,128)(2,1)} %get-tuple-element.534), channel_id=1, source_target_pairs={{2,0},{4,2},{6,4},{8,6},{10,8},{12,10},{14,12},{16,14},{18,16},{20... | collective-permute-start | bytes 1572872 | tf_op jit(solution)/shard_map/while/body/eval_jaxpr/ppermute | solution.py:18
  410.3 18.4 %collective-permute-start.3 = (bf16[4,8,64,128]{3,1,2,0:T(8,128)(2,1)}, bf16[4,8,64,128]{3,1,2,0:T(8,128)(2,1)S(1)}, u32[]{:S(2)}, u32[]{:S(2)}) collective-permute-start(bf16[4,8,64,128]{3,1,2,0:T(8,128)(2,1)} %get-tuple-element.535), channel_id=1, source_target_pairs={{0,2},{2,4},{4,6},{6,8},{8,10},{10,12},{12,14},{14,16},{16,18},{18... | collective-permute-start | bytes 1572872 | tf_op jit(solution)/shard_map/while/body/eval_jaxpr/ppermute | solution.py:17
  431.8 13.4 %collective-permute-start.2 = (bf16[4,8,64,128]{3,1,2,0:T(8,128)(2,1)}, bf16[4,8,64,128]{3,1,2,0:T(8,128)(2,1)}, u32[]{:S(2)}, u32[]{:S(2)}) collective-permute-start(bf16[4,8,64,128]{3,1,2,0:T(8,128)(2,1)} %get-tuple-element.534), channel_id=1, source_target_pairs={{2,0},{4,2},{6,4},{8,6},{10,8},{12,10},{14,12},{16,14},{18,16},{20... | collective-permute-start | bytes 1572872 | tf_op jit(solution)/shard_map/while/body/eval_jaxpr/ppermute | solution.py:18
  434.3 17.5 %collective-permute-start.3 = (bf16[4,8,64,128]{3,1,2,0:T(8,128)(2,1)}, bf16[4,8,64,128]{3,1,2,0:T(8,128)(2,1)S(1)}, u32[]{:S(2)}, u32[]{:S(2)}) collective-permute-start(bf16[4,8,64,128]{3,1,2,0:T(8,128)(2,1)} %get-tuple-element.535), channel_id=1, source_target_pairs={{0,2},{2,4},{4,6},{6,8},{8,10},{10,12},{12,14},{14,16},{16,18},{18... | collective-permute-start | bytes 1572872 | tf_op jit(solution)/shard_map/while/body/eval_jaxpr/ppermute | solution.py:17
  454.9 12.5 %collective-permute-start.2 = (bf16[4,8,64,128]{3,1,2,0:T(8,128)(2,1)}, bf16[4,8,64,128]{3,1,2,0:T(8,128)(2,1)}, u32[]{:S(2)}, u32[]{:S(2)}) collective-permute-start(bf16[4,8,64,128]{3,1,2,0:T(8,128)(2,1)} %get-tuple-element.534), channel_id=1, source_target_pairs={{2,0},{4,2},{6,4},{8,6},{10,8},{12,10},{14,12},{16,14},{18,16},{20... | collective-permute-start | bytes 1572872 | tf_op jit(solution)/shard_map/while/body/eval_jaxpr/ppermute | solution.py:18
  457.4 16.6 %collective-permute-start.3 = (bf16[4,8,64,128]{3,1,2,0:T(8,128)(2,1)}, bf16[4,8,64,128]{3,1,2,0:T(8,128)(2,1)S(1)}, u32[]{:S(2)}, u32[]{:S(2)}) collective-permute-start(bf16[4,8,64,128]{3,1,2,0:T(8,128)(2,1)} %get-tuple-element.535), channel_id=1, source_target_pairs={{0,2},{2,4},{4,6},{6,8},{8,10},{10,12},{12,14},{14,16},{16,18},{18... | collective-permute-start | bytes 1572872 | tf_op jit(solution)/shard_map/while/body/eval_jaxpr/ppermute | solution.py:17
  477.0 11.5 %collective-permute-start.2 = (bf16[4,8,64,128]{3,1,2,0:T(8,128)(2,1)}, bf16[4,8,64,128]{3,1,2,0:T(8,128)(2,1)}, u32[]{:S(2)}, u32[]{:S(2)}) collective-permute-start(bf16[4,8,64,128]{3,1,2,0:T(8,128)(2,1)} %get-tuple-element.534), channel_id=1, source_target_pairs={{2,0},{4,2},{6,4},{8,6},{10,8},{12,10},{14,12},{16,14},{18,16},{20... | collective-permute-start | bytes 1572872 | tf_op jit(solution)/shard_map/while/body/eval_jaxpr/ppermute | solution.py:18
  479.5 15.7 %collective-permute-start.3 = (bf16[4,8,64,128]{3,1,2,0:T(8,128)(2,1)}, bf16[4,8,64,128]{3,1,2,0:T(8,128)(2,1)S(1)}, u32[]{:S(2)}, u32[]{:S(2)}) collective-permute-start(bf16[4,8,64,128]{3,1,2,0:T(8,128)(2,1)} %get-tuple-element.535), channel_id=1, source_target_pairs={{0,2},{2,4},{4,6},{6,8},{8,10},{10,12},{12,14},{14,16},{16,18},{18... | collective-permute-start | bytes 1572872 | tf_op jit(solution)/shard_map/while/body/eval_jaxpr/ppermute | solution.py:17
  498.2 11.4 %collective-permute-start.2 = (bf16[4,8,64,128]{3,1,2,0:T(8,128)(2,1)}, bf16[4,8,64,128]{3,1,2,0:T(8,128)(2,1)}, u32[]{:S(2)}, u32[]{:S(2)}) collective-permute-start(bf16[4,8,64,128]{3,1,2,0:T(8,128)(2,1)} %get-tuple-element.534), channel_id=1, source_target_pairs={{2,0},{4,2},{6,4},{8,6},{10,8},{12,10},{14,12},{16,14},{18,16},{20... | collective-permute-start | bytes 1572872 | tf_op jit(solution)/shard_map/while/body/eval_jaxpr/ppermute | solution.py:18
  500.7 15.5 %collective-permute-start.3 = (bf16[4,8,64,128]{3,1,2,0:T(8,128)(2,1)}, bf16[4,8,64,128]{3,1,2,0:T(8,128)(2,1)S(1)}, u32[]{:S(2)}, u32[]{:S(2)}) collective-permute-start(bf16[4,8,64,128]{3,1,2,0:T(8,128)(2,1)} %get-tuple-element.535), channel_id=1, source_target_pairs={{0,2},{2,4},{4,6},{6,8},{8,10},{10,12},{12,14},{14,16},{16,18},{18... | collective-permute-start | bytes 1572872 | tf_op jit(solution)/shard_map/while/body/eval_jaxpr/ppermute | solution.py:17
  519.3 11.4 %collective-permute-start.2 = (bf16[4,8,64,128]{3,1,2,0:T(8,128)(2,1)}, bf16[4,8,64,128]{3,1,2,0:T(8,128)(2,1)}, u32[]{:S(2)}, u32[]{:S(2)}) collective-permute-start(bf16[4,8,64,128]{3,1,2,0:T(8,128)(2,1)} %get-tuple-element.534), channel_id=1, source_target_pairs={{2,0},{4,2},{6,4},{8,6},{10,8},{12,10},{14,12},{16,14},{18,16},{20... | collective-permute-start | bytes 1572872 | tf_op jit(solution)/shard_map/while/body/eval_jaxpr/ppermute | solution.py:18
  521.5 15.5 %collective-permute-start.3 = (bf16[4,8,64,128]{3,1,2,0:T(8,128)(2,1)}, bf16[4,8,64,128]{3,1,2,0:T(8,128)(2,1)S(1)}, u32[]{:S(2)}, u32[]{:S(2)}) collective-permute-start(bf16[4,8,64,128]{3,1,2,0:T(8,128)(2,1)} %get-tuple-element.535), channel_id=1, source_target_pairs={{0,2},{2,4},{4,6},{6,8},{8,10},{10,12},{12,14},{14,16},{16,18},{18... | collective-permute-start | bytes 1572872 | tf_op jit(solution)/shard_map/while/body/eval_jaxpr/ppermute | solution.py:17
  540.0 11.4 %collective-permute-start.2 = (bf16[4,8,64,128]{3,1,2,0:T(8,128)(2,1)}, bf16[4,8,64,128]{3,1,2,0:T(8,128)(2,1)}, u32[]{:S(2)}, u32[]{:S(2)}) collective-permute-start(bf16[4,8,64,128]{3,1,2,0:T(8,128)(2,1)} %get-tuple-element.534), channel_id=1, source_target_pairs={{2,0},{4,2},{6,4},{8,6},{10,8},{12,10},{14,12},{16,14},{18,16},{20... | collective-permute-start | bytes 1572872 | tf_op jit(solution)/shard_map/while/body/eval_jaxpr/ppermute | solution.py:18
  542.3 15.5 %collective-permute-start.3 = (bf16[4,8,64,128]{3,1,2,0:T(8,128)(2,1)}, bf16[4,8,64,128]{3,1,2,0:T(8,128)(2,1)S(1)}, u32[]{:S(2)}, u32[]{:S(2)}) collective-permute-start(bf16[4,8,64,128]{3,1,2,0:T(8,128)(2,1)} %get-tuple-element.535), channel_id=1, source_target_pairs={{0,2},{2,4},{4,6},{6,8},{8,10},{10,12},{12,14},{14,16},{16,18},{18... | collective-permute-start | bytes 1572872 | tf_op jit(solution)/shard_map/while/body/eval_jaxpr/ppermute | solution.py:17
  560.8 11.4 %collective-permute-start.2 = (bf16[4,8,64,128]{3,1,2,0:T(8,128)(2,1)}, bf16[4,8,64,128]{3,1,2,0:T(8,128)(2,1)}, u32[]{:S(2)}, u32[]{:S(2)}) collective-permute-start(bf16[4,8,64,128]{3,1,2,0:T(8,128)(2,1)} %get-tuple-element.534), channel_id=1, source_target_pairs={{2,0},{4,2},{6,4},{8,6},{10,8},{12,10},{14,12},{16,14},{18,16},{20... | collective-permute-start | bytes 1572872 | tf_op jit(solution)/shard_map/while/body/eval_jaxpr/ppermute | solution.py:18
  563.0 15.5 %collective-permute-start.3 = (bf16[4,8,64,128]{3,1,2,0:T(8,128)(2,1)}, bf16[4,8,64,128]{3,1,2,0:T(8,128)(2,1)S(1)}, u32[]{:S(2)}, u32[]{:S(2)}) collective-permute-start(bf16[4,8,64,128]{3,1,2,0:T(8,128)(2,1)} %get-tuple-element.535), channel_id=1, source_target_pairs={{0,2},{2,4},{4,6},{6,8},{8,10},{10,12},{12,14},{14,16},{16,18},{18... | collective-permute-start | bytes 1572872 | tf_op jit(solution)/shard_map/while/body/eval_jaxpr/ppermute | solution.py:17
  581.6 11.4 %collective-permute-start.2 = (bf16[4,8,64,128]{3,1,2,0:T(8,128)(2,1)}, bf16[4,8,64,128]{3,1,2,0:T(8,128)(2,1)}, u32[]{:S(2)}, u32[]{:S(2)}) collective-permute-start(bf16[4,8,64,128]{3,1,2,0:T(8,128)(2,1)} %get-tuple-element.534), channel_id=1, source_target_pairs={{2,0},{4,2},{6,4},{8,6},{10,8},{12,10},{14,12},{16,14},{18,16},{20... | collective-permute-start | bytes 1572872 | tf_op jit(solution)/shard_map/while/body/eval_jaxpr/ppermute | solution.py:18
  583.8 15.5 %collective-permute-start.3 = (bf16[4,8,64,128]{3,1,2,0:T(8,128)(2,1)}, bf16[4,8,64,128]{3,1,2,0:T(8,128)(2,1)S(1)}, u32[]{:S(2)}, u32[]{:S(2)}) collective-permute-start(bf16[4,8,64,128]{3,1,2,0:T(8,128)(2,1)} %get-tuple-element.535), channel_id=1, source_target_pairs={{0,2},{2,4},{4,6},{6,8},{8,10},{10,12},{12,14},{14,16},{16,18},{18... | collective-permute-start | bytes 1572872 | tf_op jit(solution)/shard_map/while/body/eval_jaxpr/ppermute | solution.py:17
  602.4 11.4 %collective-permute-start.2 = (bf16[4,8,64,128]{3,1,2,0:T(8,128)(2,1)}, bf16[4,8,64,128]{3,1,2,0:T(8,128)(2,1)}, u32[]{:S(2)}, u32[]{:S(2)}) collective-permute-start(bf16[4,8,64,128]{3,1,2,0:T(8,128)(2,1)} %get-tuple-element.534), channel_id=1, source_target_pairs={{2,0},{4,2},{6,4},{8,6},{10,8},{12,10},{14,12},{16,14},{18,16},{20... | collective-permute-start | bytes 1572872 | tf_op jit(solution)/shard_map/while/body/eval_jaxpr/ppermute | solution.py:18
  604.6 15.5 %collective-permute-start.3 = (bf16[4,8,64,128]{3,1,2,0:T(8,128)(2,1)}, bf16[4,8,64,128]{3,1,2,0:T(8,128)(2,1)S(1)}, u32[]{:S(2)}, u32[]{:S(2)}) collective-permute-start(bf16[4,8,64,128]{3,1,2,0:T(8,128)(2,1)} %get-tuple-element.535), channel_id=1, source_target_pairs={{0,2},{2,4},{4,6},{6,8},{8,10},{10,12},{12,14},{14,16},{16,18},{18... | collective-permute-start | bytes 1572872 | tf_op jit(solution)/shard_map/while/body/eval_jaxpr/ppermute | solution.py:17
  623.1 11.4 %collective-permute-start.2 = (bf16[4,8,64,128]{3,1,2,0:T(8,128)(2,1)}, bf16[4,8,64,128]{3,1,2,0:T(8,128)(2,1)}, u32[]{:S(2)}, u32[]{:S(2)}) collective-permute-start(bf16[4,8,64,128]{3,1,2,0:T(8,128)(2,1)} %get-tuple-element.534), channel_id=1, source_target_pairs={{2,0},{4,2},{6,4},{8,6},{10,8},{12,10},{14,12},{16,14},{18,16},{20... | collective-permute-start | bytes 1572872 | tf_op jit(solution)/shard_map/while/body/eval_jaxpr/ppermute | solution.py:18
  625.4 15.5 %collective-permute-start.3 = (bf16[4,8,64,128]{3,1,2,0:T(8,128)(2,1)}, bf16[4,8,64,128]{3,1,2,0:T(8,128)(2,1)S(1)}, u32[]{:S(2)}, u32[]{:S(2)}) collective-permute-start(bf16[4,8,64,128]{3,1,2,0:T(8,128)(2,1)} %get-tuple-element.535), channel_id=1, source_target_pairs={{0,2},{2,4},{4,6},{6,8},{8,10},{10,12},{12,14},{14,16},{16,18},{18... | collective-permute-start | bytes 1572872 | tf_op jit(solution)/shard_map/while/body/eval_jaxpr/ppermute | solution.py:17
  643.9 11.7 %collective-permute-start.2 = (bf16[4,8,64,128]{3,1,2,0:T(8,128)(2,1)}, bf16[4,8,64,128]{3,1,2,0:T(8,128)(2,1)}, u32[]{:S(2)}, u32[]{:S(2)}) collective-permute-start(bf16[4,8,64,128]{3,1,2,0:T(8,128)(2,1)} %get-tuple-element.534), channel_id=1, source_target_pairs={{2,0},{4,2},{6,4},{8,6},{10,8},{12,10},{14,12},{16,14},{18,16},{20... | collective-permute-start | bytes 1572872 | tf_op jit(solution)/shard_map/while/body/eval_jaxpr/ppermute | solution.py:18
  646.1 15.9 %collective-permute-start.3 = (bf16[4,8,64,128]{3,1,2,0:T(8,128)(2,1)}, bf16[4,8,64,128]{3,1,2,0:T(8,128)(2,1)S(1)}, u32[]{:S(2)}, u32[]{:S(2)}) collective-permute-start(bf16[4,8,64,128]{3,1,2,0:T(8,128)(2,1)} %get-tuple-element.535), channel_id=1, source_target_pairs={{0,2},{2,4},{4,6},{6,8},{8,10},{10,12},{12,14},{14,16},{16,18},{18... | collective-permute-start | bytes 1572872 | tf_op jit(solution)/shard_map/while/body/eval_jaxpr/ppermute | solution.py:17
  665.0 12.8 %collective-permute-start.2 = (bf16[4,8,64,128]{3,1,2,0:T(8,128)(2,1)}, bf16[4,8,64,128]{3,1,2,0:T(8,128)(2,1)}, u32[]{:S(2)}, u32[]{:S(2)}) collective-permute-start(bf16[4,8,64,128]{3,1,2,0:T(8,128)(2,1)} %get-tuple-element.534), channel_id=1, source_target_pairs={{2,0},{4,2},{6,4},{8,6},{10,8},{12,10},{14,12},{16,14},{18,16},{20... | collective-permute-start | bytes 1572872 | tf_op jit(solution)/shard_map/while/body/eval_jaxpr/ppermute | solution.py:18
  667.0 16.9 %collective-permute-start.3 = (bf16[4,8,64,128]{3,1,2,0:T(8,128)(2,1)}, bf16[4,8,64,128]{3,1,2,0:T(8,128)(2,1)S(1)}, u32[]{:S(2)}, u32[]{:S(2)}) collective-permute-start(bf16[4,8,64,128]{3,1,2,0:T(8,128)(2,1)} %get-tuple-element.535), channel_id=1, source_target_pairs={{0,2},{2,4},{4,6},{6,8},{8,10},{10,12},{12,14},{14,16},{16,18},{18... | collective-permute-start | bytes 1572872 | tf_op jit(solution)/shard_map/while/body/eval_jaxpr/ppermute | solution.py:17
  687.0 11.4 %collective-permute-start.2 = (bf16[4,8,64,128]{3,1,2,0:T(8,128)(2,1)}, bf16[4,8,64,128]{3,1,2,0:T(8,128)(2,1)}, u32[]{:S(2)}, u32[]{:S(2)}) collective-permute-start(bf16[4,8,64,128]{3,1,2,0:T(8,128)(2,1)} %get-tuple-element.534), channel_id=1, source_target_pairs={{2,0},{4,2},{6,4},{8,6},{10,8},{12,10},{14,12},{16,14},{18,16},{20... | collective-permute-start | bytes 1572872 | tf_op jit(solution)/shard_map/while/body/eval_jaxpr/ppermute | solution.py:18
  688.9 15.5 %collective-permute-start.3 = (bf16[4,8,64,128]{3,1,2,0:T(8,128)(2,1)}, bf16[4,8,64,128]{3,1,2,0:T(8,128)(2,1)S(1)}, u32[]{:S(2)}, u32[]{:S(2)}) collective-permute-start(bf16[4,8,64,128]{3,1,2,0:T(8,128)(2,1)} %get-tuple-element.535), channel_id=1, source_target_pairs={{0,2},{2,4},{4,6},{6,8},{8,10},{10,12},{12,14},{14,16},{16,18},{18... | collective-permute-start | bytes 1572872 | tf_op jit(solution)/shard_map/while/body/eval_jaxpr/ppermute | solution.py:17
  (46 other events, 448.3 us)
Sparse Core Ops, SparseCore 0:
  319.6 31.3 all-reduce.2
where the time goes:
time: 718 us; the launch traced here: 715 us
  starting transfers between devices  291 us (41%)
  waiting for transfers between devices  218 us (30%)
  matrix products  104 us (14%)
  local copies, waits for them, and re-layouts  52.6 us (7%)
  other arithmetic  29.2 us (4%)
  between operations  14.3 us (2%)
    ppermute x35, starting transfers between devices, extended_2(): after = lax.ppermute(initial, axis, down)  198 us
    ppermute x35, waiting for transfers between devices, extended_2(): after = lax.ppermute(initial, axis, down)  132 us
    ppermute x35, starting transfers between devices, extended_2(): before = lax.ppermute(last, axis, up)  92.9 us
    ppermute x35, waiting for transfers between devices, extended_2(): before = lax.ppermute(last, axis, up)  78.4 us
    dot_general x16, matrix products, coupling(): jnp.einsum('bnm,bmec->bnec', cross_next, lower.astype(jnp.float32), preci...  33.9 us
    dot_general x16, matrix products, coupling(): jnp.einsum('bnm,bmec->bnec', cross_own, state_float[:, :, patch_side:], p...  24.5 us
    convert_element_type x16, other arithmetic, renew(): jnp.where(chosen, jnp.where(support_grid, proposal, 0.0), state_float)  21.9 us
    slice x17, local copies, waits for them, and re-layouts, extended_2(): last = lax.slice_in_dim(value, length - width, length, axis=dim)  21.6 us
  transfers between devices with their start and end apart: 71, of which 51 were waited for; matrix products, arithmetic and copies ran while one was open for 12% of the time, Pallas kernels for 0%

commit v1 on v0

v1 whole, which is shorter than its diff:
```python
import functools

import jax
import jax.numpy as jnp
from jax import lax
from jax.experimental import pallas as pl
from jax.experimental.pallas import tpu as pltpu
from jax.sharding import PartitionSpec as P

exact = lax.Precision.HIGHEST
f32 = jnp.float32
bf16 = jnp.bfloat16
BINS = 4
LAYERS = 8
SLOTS = 32
COLOURS = 16
PATCH = 64
HALF = 32
EDGE = 128
FRAMES = 128
GROUP = BINS * COLOURS
floor_share = 0.25

vmem = pl.BlockSpec(memory_space=pltpu.VMEM)
smem = pl.BlockSpec(memory_space=pltpu.SMEM)


def iota(shape, dim):
    return lax.broadcasted_iota(jnp.int32, shape, dim)


def dot_nt(a, b, precision=None):
    return lax.dot_general(
        a, b, (((1,), (1,)), ((), ())), precision=precision, preferred_element_type=f32
    )


def dot(a, b, precision=None):
    return lax.dot_general(
        a, b, (((1,), (0,)), ((), ())), precision=precision, preferred_element_type=f32
    )


def neighbour_tile(tile, core, tiles):
    other = jnp.where(core == 0, tile - 1, tile + 1)
    other = jnp.where(other < 0, tile + 1, other)
    return jnp.where(other >= tiles, tile - 1, other)


def slab_kernel(rows_ref, cols_ref, live_ref, patches_ref, out_ref, own_ref):
    core = lax.axis_index("frame")
    line = iota((PATCH, PATCH), 0)
    base_out = jnp.where(core == 0, 0, 96)
    base_own = jnp.where(core == 0, 32, 64)
    row_at = jnp.where(line < HALF, base_out + line, base_own + line - HALF) - HALF
    row_at = row_at - iota((PATCH, PATCH), 1)
    col_at = iota((PATCH, EDGE), 1) - iota((PATCH, EDGE), 0)
    for s in range(SLOTS):
        live = live_ref[s] > 0
        row_pick = jnp.where((row_at == rows_ref[s]) & live, 1.0, 0.0).astype(bf16)
        col_pick = jnp.where(col_at == cols_ref[s], 1.0, 0.0).astype(bf16)
        placed = dot(row_pick, patches_ref[s]).astype(bf16)
        spread = dot(placed, col_pick).astype(bf16)
        out_ref[s] = spread[:HALF]
        own_ref[s] = spread[HALF:]


def partial_kernel(
    tiles, core_ref, colour_ref, live_ref, mine_ref, other_ref, own_ref, recv_ref,
    near_ref, far_ref, slab_ref, message_ref, live_rows_ref,
):
    tile = lax.axis_index("tile")
    core = lax.axis_index("frame")
    beside = neighbour_tile(tile, core, tiles)
    message_ref[...] = jnp.zeros_like(message_ref)
    live_rows_ref[...] = jnp.zeros_like(live_rows_ref)
    start = GROUP + COLOURS
    wide = jnp.concatenate([near_ref[...], far_ref[...]], axis=1)
    swapped = jnp.concatenate([far_ref[...], near_ref[...]], axis=1)
    first = jnp.where(core == 0, wide, swapped)
    for s in range(SLOTS):
        b = s // LAYERS
        mine = b * COLOURS + colour_ref[tile * SLOTS + s]
        theirs = b * COLOURS + colour_ref[beside * SLOTS + s]
        slab_ref[mine] = own_ref[s]
        slab_ref[theirs] = recv_ref[s]
        alive = live_ref[s].astype(f32)
        message_ref[pl.ds(start + mine, 1), :] = first[s : s + 1] * alive
        live_rows_ref[pl.ds(mine, 1), :] = jnp.full((1, FRAMES), alive, f32)
    same_row = iota((1024, 256), 0) % 16 == iota((1024, 256), 1) % 16
    fold = jnp.where(iota((COLOURS, 256), 1) // 16 == iota((COLOURS, 256), 0), 1.0, 0.0)
    gram = jnp.zeros((COLOURS, EDGE), f32)
    for b in range(BINS):
        lanes = slice(b * EDGE, (b + 1) * EDGE)
        both = [
            slab_ref[b * COLOURS : (b + 1) * COLOURS, 16 * q : 16 * q + 16, :].reshape(256, EDGE)
            for q in range(2)
        ]
        both = jnp.concatenate(both, axis=1)
        parts = []
        for ref in (mine_ref, other_ref):
            pixels = [ref[:, 16 * q : 16 * q + 16, lanes].reshape(1024, EDGE) for q in range(2)]
            pixels = jnp.concatenate(pixels, axis=1)
            product = jnp.where(same_row, dot_nt(pixels, both), 0.0)
            parts.append(jnp.sum(product.reshape(64, 16, 256), axis=1))
        near = jnp.concatenate(parts, axis=0)
        far = jnp.concatenate(parts[::-1], axis=0)
        ordered = jnp.where(core == 0, near, far)
        message_ref[b * COLOURS : (b + 1) * COLOURS, :] = dot_nt(fold, ordered, exact)
        square = jnp.where(same_row[:256], dot_nt(both, both), 0.0)
        square = jnp.sum(square.reshape(COLOURS, 16, 256), axis=1)
        spread = iota((256, EDGE), 0) // 16 + b * COLOURS == iota((256, EDGE), 1)
        gram = gram + dot(square, jnp.where(spread, 1.0, 0.0), exact)
    message_ref[GROUP : GROUP + COLOURS, :] = gram


def block_diagonal(gram):
    tall = jnp.concatenate([gram] * BINS, axis=0)[:, :GROUP]
    keep = iota((GROUP, GROUP), 0) // COLOURS == iota((GROUP, GROUP), 1) // COLOURS
    return jnp.where(keep, tall, 0.0)


def join_kernel(mine_ref, pair_ref, out_ref, start_ref):
    grams = slice(GROUP, GROUP + COLOURS)
    traces = slice(GROUP + COLOURS, 2 * GROUP + COLOURS)
    gram = mine_ref[grams, :] + pair_ref[grams, :]
    current = mine_ref[traces, :] + pair_ref[traces, :]
    drive = mine_ref[:GROUP, :] + pair_ref[:GROUP, :]
    out_ref[:GROUP, :] = drive - dot(block_diagonal(gram), current, exact)
    out_ref[grams, :] = gram
    start_ref[...] = mine_ref[traces, :]


def settle(phase_ref, live_ref, gram, residual, current, phase, state_ref, change_ref):
    whole = jnp.concatenate([gram] * BINS, axis=0)
    lane = iota((GROUP, EDGE), 1)
    diag = jnp.sum(jnp.where(lane == iota((GROUP, EDGE), 0), whole, 0.0), axis=1, keepdims=True)
    inverse = 1.0 / (diag + (1.0 - live_ref[...]))
    chosen = phase_ref[...] == phase
    news = []
    changes = []
    for b in range(BINS):
        rows = slice(b * COLOURS, (b + 1) * COLOURS)
        rest, now = residual[rows], current[rows]
        inv, pick = inverse[rows], chosen[rows]
        row_id = iota((COLOURS, FRAMES), 0)
        change = jnp.zeros((COLOURS, FRAMES), f32)
        for g in range(COLOURS):
            at = slice(g, g + 1)
            value = jnp.maximum(now[at] + rest[at] * inv[at], 0.0) - now[at]
            delta = jnp.where(pick[at], value, 0.0)
            lane_at = slice(b * COLOURS + g, b * COLOURS + g + 1)
            column = jnp.broadcast_to(gram[:, lane_at], (COLOURS, FRAMES))
            rest = rest - column * delta
            change = jnp.where(row_id == g, delta, change)
        state_ref[rows, :] = rest
        state_ref[GROUP + b * COLOURS : GROUP + (b + 1) * COLOURS, :] = now + change
        change_ref[rows, :] = change


def first_phase_kernel(phase_ref, live_ref, start_ref, here_ref, there_ref, state_ref, change_ref):
    grams = slice(GROUP, GROUP + COLOURS)
    gram = here_ref[grams, :] + there_ref[grams, :]
    residual = here_ref[:GROUP, :] + there_ref[:GROUP, :]
    settle(phase_ref, live_ref, gram, residual, start_ref[...], 0, state_ref, change_ref)


def relay_kernel(here_ref, delta_ref, out_ref):
    grams = slice(GROUP, GROUP + COLOURS)
    out_ref[...] = dot(block_diagonal(here_ref[grams, :]), delta_ref[...], exact)


def next_phase_kernel(
    step_ref, phase_ref, live_ref, here_ref, there_ref, mine_ref, other_ref, old_ref, beside_ref,
    delta_ref, state_ref, change_ref, beside_out_ref,
):
    grams = slice(GROUP, GROUP + COLOURS)
    gram = here_ref[grams, :] + there_ref[grams, :]
    residual = old_ref[:GROUP, :] - (mine_ref[...] + other_ref[...])
    current = old_ref[GROUP:, :]
    beside_out_ref[...] = beside_ref[...] + delta_ref[...]
    settle(phase_ref, live_ref, gram, residual, current, step_ref[0], state_ref, change_ref)


def spatial_kernel(
    tiles, core_ref, colour_ref, mine_ref, other_ref, slab_ref, state_in_ref, beside_ref, delta_ref,
    traces_ref, out_ref, own_ref, weight_ref, cross_ref, field_ref, state_ref,
):
    tile = lax.axis_index("tile")
    core = lax.axis_index("frame")
    beside = neighbour_tile(tile, core, tiles)
    own = state_in_ref[GROUP:, :]
    rolled = jnp.concatenate([own[:, 64:], own[:, :64]], axis=1)
    framed = jnp.where(core == 0, own, rolled)[:, :64]
    cross_ref[:GROUP, :64] = framed
    for s in range(SLOTS):
        at = (s // LAYERS) * COLOURS + colour_ref[tile * SLOTS + s]
        traces_ref[s : s + 1, :] = cross_ref[pl.ds(at, 1), :64]
    both = own + beside_ref[...] + delta_ref[...]
    position = (iota((FRAMES, 2048), 1) // 16 + 64 * core) % FRAMES
    repeat = jnp.where(position == iota((FRAMES, 2048), 0), 1.0, 0.0).astype(bf16)
    repeated = dot(both.astype(bf16), repeat)
    same_row = iota((16, 2048), 0) == iota((16, 2048), 1) % 16
    for b in range(BINS):
        rows = slice(b * COLOURS, (b + 1) * COLOURS)
        lanes = slice(b * EDGE, (b + 1) * EDGE)
        for g in range(COLOURS):
            line = repeated[b * COLOURS + g : b * COLOURS + g + 1]
            weight_ref[16 * g : 16 * g + 16, :] = jnp.where(same_row, line, 0.0).astype(bf16)
        pixels = []
        for ref in (mine_ref, other_ref):
            part = [ref[:, 16 * q : 16 * q + 16, lanes].reshape(1024, EDGE) for q in range(2)]
            pixels.append(jnp.concatenate(part, axis=1))
        field_ref[b] = dot(weight_ref[...], jnp.concatenate(pixels, axis=0))
        now = both[rows]
        cross = dot_nt(now, now, exact)
        for g in range(COLOURS):
            column = jnp.broadcast_to(cross[:, g : g + 1], (COLOURS, EDGE))
            cross_ref[(b * COLOURS + g) * 16 : (b * COLOURS + g) * 16 + 16, :] = column

    floor = floor_share * FRAMES

    def update(step, carry):
        b = step // 2
        q = step % 2
        first = b * COLOURS
        row = pl.multiple_of(q * 16, 16)
        states = [
            slab_ref[first + m, pl.ds(row, 16), :].astype(f32) for m in range(COLOURS)
        ]
        for g in range(COLOURS):
            base = (first + g) * 16
            support = states[g] > 0.0
            mixed = jnp.zeros((16, EDGE), f32)
            for m in range(COLOURS):
                mixed = mixed + cross_ref[pl.ds(base + m, 1), :] * states[m]
            scale = 1.0 / jnp.maximum(cross_ref[pl.ds(base + g, 1), :], floor)
            lane = pl.multiple_of(q * EDGE, EDGE)
            field = field_ref[b, 16 * g : 16 * g + 16, pl.ds(lane, EDGE)]
            fresh = jnp.maximum(states[g] + (field - mixed) * scale, 0.0)
            fresh = jnp.where(support, fresh, 0.0).astype(bf16)
            state_ref[first + g, pl.ds(row, 16), :] = fresh
            states[g] = fresh.astype(f32)
        return carry

    lax.fori_loop(0, 2 * BINS, update, 0)
    for s in range(SLOTS):
        first = (s // LAYERS) * COLOURS
        own_ref[s] = state_ref[first + colour_ref[tile * SLOTS + s]]
        out_ref[s] = state_ref[first + colour_ref[beside * SLOTS + s]]


def patch_kernel(rows_ref, cols_ref, own_ref, recv_ref, sib_own_ref, sib_recv_ref, out_ref):
    core = lax.axis_index("frame")
    line = iota((PATCH, EDGE), 1)
    block = line // HALF
    home = jnp.where(core == 0, HALF, 2 * HALF)
    edge = jnp.where(core == 0, 0, 3 * HALF)
    far_home = 3 * HALF - home
    far_edge = 3 * HALF - edge
    base = jnp.where(block == 0, home, jnp.where(block == 1, edge, jnp.where(block == 2, far_home, far_edge)))
    row_at = base + line % HALF - HALF - iota((PATCH, EDGE), 0)
    col_at = iota((EDGE, PATCH), 0) - iota((EDGE, PATCH), 1)
    for s in range(SLOTS):
        row_pick = jnp.where(row_at == rows_ref[s], 1.0, 0.0).astype(bf16)
        col_pick = jnp.where(col_at == cols_ref[s], 1.0, 0.0).astype(bf16)
        whole = jnp.concatenate([own_ref[s], recv_ref[s], sib_own_ref[s], sib_recv_ref[s]], axis=0)
        lifted = dot(row_pick, whole).astype(bf16)
        out_ref[s] = dot(lifted, col_pick).astype(bf16)


def shape(dims, dtype=f32):
    return jax.ShapeDtypeStruct(dims, dtype)


def call(kernel, ins, outs, name, scratch=(), limit=None):
    return pl.pallas_call(
        kernel,
        in_specs=ins,
        out_specs=[vmem] * len(outs),
        out_shape=outs,
        scratch_shapes=list(scratch),
        name=name,
        compiler_params=pltpu.CompilerParams(vmem_limit_bytes=limit) if limit else None,
    )


def on_device(movie_block, patches, patch_rows, patch_cols, neuron_live, neuron_colour, traces):
    tiles = lax.axis_size("tile")
    core = lax.axis_index("frame")
    tile = lax.axis_index("tile")
    swap_pairs = []
    for t in range(tiles - 1):
        swap_pairs += [(2 * t + 1, 2 * t + 2), (2 * t + 2, 2 * t + 1)]

    def pair_swap(value):
        return lax.ppermute(value, ("tile", "frame"), swap_pairs)

    def chip_swap(value):
        return lax.ppermute(value, "frame", [(0, 1), (1, 0)])

    own_colour = lax.dynamic_slice_in_dim(neuron_colour, tile * SLOTS, SLOTS)
    owned = jnp.any(
        own_colour.reshape(BINS, LAYERS, 1) == jnp.arange(COLOURS, dtype=jnp.int32), axis=1
    )
    turns = (owned[:, 1:] != owned[:, :-1]).astype(jnp.int32)
    later = jnp.arange(COLOURS)[None, :] > jnp.arange(COLOURS - 1)[:, None]
    phase_of = jnp.sum(jnp.where(later[None], turns[:, :, None], 0), axis=1)
    phase_count = jnp.max(jnp.sum(turns, axis=1)) + 1
    phases = jnp.where(owned, phase_of, -1).reshape(GROUP, 1)
    phases = jnp.broadcast_to(phases, (GROUP, FRAMES))

    movie_out = lax.dynamic_slice_in_dim(movie_block, HALF * (1 - core), HALF, 1)
    movie_other = chip_swap(movie_out)
    traces_other = chip_swap(traces)

    piece_out, piece_own = call(
        slab_kernel,
        [smem, smem, smem, vmem],
        [shape((SLOTS, HALF, EDGE), bf16)] * 2,
        "slabs",
    )(patch_rows, patch_cols, neuron_live, patches)
    piece_recv = pair_swap(piece_out)

    core_at = core.reshape(1)
    movie_spec = pl.BlockSpec((64, HALF, 512), lambda i, c: (0, c[0], 0))
    whole2 = lambda dims: pl.BlockSpec(dims, lambda i, c: (0,) * len(dims))
    smem_in = pl.BlockSpec(memory_space=pltpu.SMEM)

    slab, message, live_rows = pl.pallas_call(
        functools.partial(partial_kernel, tiles),
        grid_spec=pltpu.PrefetchScalarGridSpec(
            num_scalar_prefetch=1,
            grid=(1,),
            in_specs=[
                smem_in, smem_in, movie_spec, whole2((64, HALF, 512)), whole2((SLOTS, HALF, EDGE)),
                whole2((SLOTS, HALF, EDGE)), whole2((SLOTS, 64)), whole2((SLOTS, 64)),
            ],
            out_specs=[
                whole2((GROUP, HALF, EDGE)), whole2((2 * GROUP + COLOURS, FRAMES)),
                whole2((GROUP, FRAMES)),
            ],
        ),
        out_shape=[
            shape((GROUP, HALF, EDGE), bf16), shape((2 * GROUP + COLOURS, FRAMES)),
            shape((GROUP, FRAMES)),
        ],
        compiler_params=pltpu.CompilerParams(vmem_limit_bytes=40 * 2**20),
        name="partial_sums",
    )(
        core_at, neuron_colour, neuron_live, movie_block, movie_other, piece_own, piece_recv,
        traces, traces_other,
    )

    message_pair = pair_swap(message)
    here, start = call(
        join_kernel, [vmem] * 2, [shape((GROUP + COLOURS, FRAMES)), shape((GROUP, FRAMES))], "join"
    )(message, message_pair)
    there = chip_swap(here)
    beside = message_pair[GROUP + COLOURS :]
    state_shapes = [shape((2 * GROUP, FRAMES)), shape((GROUP, FRAMES))]
    state, change = call(first_phase_kernel, [vmem] * 5, state_shapes, "first_phase")(
        phases, live_rows, start, here, there
    )

    def advance(carry):
        step, state, beside, change = carry
        delta = pair_swap(change)
        (mine,) = call(relay_kernel, [vmem] * 2, [shape((GROUP, FRAMES))], "relay")(here, delta)
        other = chip_swap(mine)
        state, change, beside = call(
            next_phase_kernel, [smem] + [vmem] * 9, state_shapes + [shape((GROUP, FRAMES))], "next_phase"
        )(step.reshape(1), phases, live_rows, here, there, mine, other, state, beside, delta)
        return step + 1, state, beside, change

    carry = advance((jnp.int32(1), state, beside, change))
    _, state, beside, change = lax.while_loop(lambda c: c[0] < phase_count, advance, carry)
    delta = pair_swap(change)

    new_traces, final_out, final_own = pl.pallas_call(
        functools.partial(spatial_kernel, tiles),
        grid_spec=pltpu.PrefetchScalarGridSpec(
            num_scalar_prefetch=1,
            grid=(1,),
            in_specs=[
                smem_in, movie_spec, whole2((64, HALF, 512)), whole2((GROUP, HALF, EDGE)),
                whole2((2 * GROUP, FRAMES)), whole2((GROUP, FRAMES)), whole2((GROUP, FRAMES)),
            ],
            out_specs=[whole2((SLOTS, 64)), whole2((SLOTS, HALF, EDGE)), whole2((SLOTS, HALF, EDGE))],
            scratch_shapes=[
                pltpu.VMEM((256, 2048), bf16),
                pltpu.VMEM((GROUP * COLOURS, EDGE), f32),
                pltpu.VMEM((BINS, 256, 256), f32),
                pltpu.VMEM((GROUP, HALF, EDGE), bf16),
            ],
        ),
        out_shape=[
            shape((SLOTS, 64)), shape((SLOTS, HALF, EDGE), bf16), shape((SLOTS, HALF, EDGE), bf16)
        ],
        compiler_params=pltpu.CompilerParams(vmem_limit_bytes=40 * 2**20),
        name="spatial",
    )(core_at, neuron_colour, movie_block, movie_other, slab, state, beside, delta)

    far_own = chip_swap(final_own)
    final_recv = pair_swap(final_out)
    far_recv = chip_swap(final_recv)
    (new_patches,) = call(
        patch_kernel, [smem, smem] + [vmem] * 4, [shape((SLOTS, PATCH, PATCH), bf16)], "patches"
    )(patch_rows, patch_cols, final_own, final_recv, far_own, far_recv)
    return (new_traces, new_patches)


def solution(mesh):
    placed = (
        P("frame", "tile", None),
        P("tile", None, None),
        P("tile"),
        P("tile"),
        P("tile"),
        P(),
        P("tile", "frame"),
    )
    return jax.shard_map(
        on_device,
        mesh=mesh,
        in_specs=placed,
        out_specs=(P("tile", "frame"), P("tile", None, None)),
        check_vma=False,
    )
```

time: 718 us -> 95.8 us (0.13)
  starting transfers between devices: 291 us -> 42 us
  waiting for transfers between devices: 218 us -> 15.9 us
  matrix products: 104 us -> 0 us
  local copies, waits for them, and re-layouts: 52.6 us -> 13.5 us
  other arithmetic: 29.2 us -> 1.09 us
  Pallas kernels: 0 us -> 20.8 us
  between operations: 14.3 us -> 1.46 us
    ppermute x70 -> x11, starting transfers between devices: 291 us -> 42 us  [the longest x5 41.8 us: pair_swap(): return lax.ppermute(value, ('tile', 'frame'), swap_pairs)]
    ppermute x70 -> x11, waiting for transfers between devices: 210 us -> 15.9 us  [the longest x5 12.5 us: pair_swap(): return lax.ppermute(value, ('tile', 'frame'), swap_pairs)]
    dot_general x122 -> x0, matrix products: 104 us -> none  [the longest x16 33.9 us: coupling(): jnp.einsum('bnm,bmec->bnec', cross_next, lower.astype(jnp.float32), preci...]
    convert_element_type x17 -> x1, other arithmetic: 21.9 us -> 0.08 us  [on_device(): turns = (owned[:, 1:] != owned[:, :-1]).astype(jnp.int32)]
    slice x18 -> x1, local copies, waits for them, and re-layouts: 22.5 us -> 1.38 us  [on_device(): beside = message_pair[GROUP + COLOURS:]]
    pallas_call x0 -> x8, Pallas kernels: none -> 20.8 us  [the longest x1 5.35 us: on_device(): pl.pallas_call(functools.partial(spatial_kernel, tiles), grid_spec=pltpu....]
    reshape x4 -> x0, local copies, waits for them, and re-layouts: 15 us -> none  [the longest x1 13.5 us: on_device(): extended.reshape(frames_dev, slab_edge, bin_count, slab_edge)]
    concatenate x1 -> x0, local copies, waits for them, and re-layouts: 12 us -> none  [extended_2(): value = jnp.concatenate([before, value, after], axis=dim)]
  transfers between devices with their start and end apart: 71 -> 11, of which waited for: 51 -> 8; matrix products, arithmetic and copies ran while one was open for 12% -> 3% of each run, Pallas kernels for 0% -> 2%
where the time goes in v1:
time: 95.8 us; the launch traced here: 94.8 us
  starting transfers between devices  42 us (44%)
  Pallas kernels  20.8 us (22%)
  waiting for transfers between devices  15.9 us (17%)
  local copies, waits for them, and re-layouts  13.5 us (14%)
  between operations  1.46 us (2%)
  other arithmetic  1.09 us (1%)
    ppermute x5, starting transfers between devices, pair_swap(): return lax.ppermute(value, ('tile', 'frame'), swap_pairs)  41.8 us
    ppermute x5, waiting for transfers between devices, pair_swap(): return lax.ppermute(value, ('tile', 'frame'), swap_pairs)  12.5 us
    unnamed x28, local copies, waits for them, and re-layouts  7.89 us
    pallas_call x1, Pallas kernels, on_device(): pl.pallas_call(functools.partial(spatial_kernel, tiles), grid_spec=pltpu....  5.35 us
    pallas_call x1, Pallas kernels, on_device(): pl.pallas_call(functools.partial(partial_kernel, tiles), grid_spec=pltpu....  4.37 us
    ppermute x6, waiting for transfers between devices, chip_swap(): return lax.ppermute(value, 'frame', [(0, 1), (1, 0)])  3.37 us
    dynamic_slice x1, local copies, waits for them, and re-layouts, on_device(): lax.dynamic_slice_in_dim(movie_block, HALF * (1 - core), HALF, 1)  3.2 us
    pallas_call x1, Pallas kernels, on_device(): call(patch_kernel, [smem, smem] + [vmem] * 4, [shape((SLOTS, PATCH, PATCH...  2.77 us
  transfers between devices with their start and end apart: 11, of which 8 were waited for; matrix products, arithmetic and copies ran while one was open for 3% of the time, Pallas kernels for 2%

profile of v1, /device:TPU:6, one launch (start us, length us, event | category | flops | bytes accessed | tf_op | source)
XLA Modules:
  0.0 94.8 jit_solution(11837965214918755956)
XLA Ops:
  0.7 0.0 copy-start.7
  0.7 3.2 %constant_dynamic-slice_fusion = bf16[64,32,512]{2,1,0:T(8,128)(2,1)} fusion(bf16[64,64,512]{2,1,0:T(8,128)(2,1)} %mine_ref.3, s32[]{:T(128)S(6)} %select_n.21), kind=kLoop, calls=%fused_computation.7 | loop fusion | bytes 4194308 | tf_op jit(solution)/shard_map/dynamic_slice | solution.py:313
  3.9 2.4 %slabs.1 = (bf16[32,32,128]{2,1,0:T(8,128)(2,1)}, bf16[32,32,128]{2,1,0:T(8,128)(2,1)}) custom-call(s32[32]{0:T(128)} %rows_ref.3, s32[32]{0:T(128)} %cols_ref.3, s32[32]{0:T(128)} %live_ref.3, bf16[32,64,64]{2,1,0:T(8,128)(2,1)} %patches_ref.1), custom_call_target="tpu_custom_call" | custom-call | tf_op jit(solution)/shard_map/slabs/pallas_call | solution.py:317
  6.2 10.6 %collective-permute-start.3 = (bf16[32,32,128]{2,1,0:T(8,128)(2,1)}, bf16[32,32,128]{2,1,0:T(8,128)(2,1)S(1)}, u32[]{:S(2)}, u32[]{:S(2)}) collective-permute-start(bf16[32,32,128]{2,1,0:T(8,128)(2,1)} %get-tuple-element.71), channel_id=1, source_target_pairs={{1,2},{2,1},{3,4},{4,3},{5,6},{6,5},{7,8},{8,7},{9,10},{10,9},{11,... | collective-permute-start | bytes 786440 | tf_op jit(solution)/shard_map/ppermute | solution.py:297
  16.8 0.1 collective-permute-start.4
  16.9 0.1 dynamic_slice.7
  17.0 0.1 eq.15
  17.1 0.1 fusion.2
  17.2 0.1 compare_convert_fusion
  17.3 0.1 copy.9
  17.4 0.7 collective-permute-done.4.far_ref
  18.1 3.0 %collective-permute-done.3.recv_ref = bf16[32,32,128]{2,1,0:T(8,128)(2,1)S(1)} collective-permute-done((bf16[32,32,128]{2,1,0:T(8,128)(2,1)}, bf16[32,32,128]{2,1,0:T(8,128)(2,1)S(1)}, u32[]{:S(2)}, u32[]{:S(2)}) %collective-permute-start.3) | collective-permute-done | bytes 262176 | tf_op jit(solution)/shard_map/ppermute | solution.py:297
  21.1 0.0 collective-permute-done.2.other_ref
  21.1 2.2 %copy-done = bf16[64,64,512]{2,1,0:T(8,128)(2,1)S(1)} copy-done((bf16[64,64,512]{2,1,0:T(8,128)(2,1)S(1)}, bf16[64,64,512]{2,1,0:T(8,128)(2,1)}, u32[]{:S(2)}) %copy-start) | copy-done | bytes 4194328
  23.3 0.9 %copy-done.2 = bf16[32,32,128]{2,1,0:T(8,128)(2,1)S(1)} copy-done((bf16[32,32,128]{2,1,0:T(8,128)(2,1)S(1)}, bf16[32,32,128]{2,1,0:T(8,128)(2,1)}, u32[]{:S(2)}) %copy-start.2) | copy-done | bytes 262168
  24.2 4.4 %partial_sums.1 = (bf16[64,32,128]{2,1,0:T(8,128)(2,1)S(1)}, f32[144,128]{1,0:T(8,128)S(1)}, f32[64,128]{1,0:T(8,128)S(1)}) custom-call(s32[1]{0:T(128)} %bitcast.core_ref, s32[4096]{0:T(1024)S(1)} %copy-done.5, s32[32]{0:T(128)S(1)} %copy-done.7, bf16[64,64,512]{2,1,0:T(8,128)(2,1)S(1)} %copy-done, ...), custom_call_target="tpu_custom_call" | custom-call | tf_op jit(solution)/shard_map/partial_sums/pallas_call | solution.py:330
  28.6 7.9 %collective-permute-start.5 = (f32[144,128]{1,0:T(8,128)S(1)}, f32[144,128]{1,0:T(8,128)S(1)}, u32[]{:S(2)}, u32[]{:S(2)}) collective-permute-start(f32[144,128]{1,0:T(8,128)S(1)} %get-tuple-element.74.mine_ref), channel_id=1, source_target_pairs={{1,2},{2,1},{3,4},{4,3},{5,6},{6,5},{7,8},{8,7},{9,10},{10,9},{11,... | collective-permute-start | bytes 221192 | tf_op jit(solution)/shard_map/ppermute | solution.py:297
  36.5 0.1 select_reduce_fusion
  36.6 1.9 %collective-permute-done.5.pair_ref = f32[144,128]{1,0:T(8,128)S(1)} collective-permute-done((f32[144,128]{1,0:T(8,128)S(1)}, f32[144,128]{1,0:T(8,128)S(1)}, u32[]{:S(2)}, u32[]{:S(2)}) %collective-permute-start.5) | collective-permute-done | bytes 73760 | tf_op jit(solution)/shard_map/ppermute | solution.py:297
  38.5 0.6 copy-done.13
  39.1 1.5 %join.1 = (f32[80,128]{1,0:T(8,128)S(1)}, f32[64,128]{1,0:T(8,128)}) custom-call(f32[144,128]{1,0:T(8,128)} %copy-done.4, f32[144,128]{1,0:T(8,128)} %copy-done.13), custom_call_target="tpu_custom_call" | custom-call | tf_op jit(solution)/shard_map/join/pallas_call | solution.py:356
  40.7 0.0 collective-permute-start.6
  40.7 0.1 select_n.25
  40.7 1.1 %collective-permute-done.6.there_ref = f32[80,128]{1,0:T(8,128)S(1)} collective-permute-done((f32[80,128]{1,0:T(8,128)S(1)}, f32[80,128]{1,0:T(8,128)S(1)}, u32[]{:S(2)}, u32[]{:S(2)}) %collective-permute-start.6) | collective-permute-done | bytes 40992 | tf_op jit(solution)/shard_map/ppermute | solution.py:300
  41.9 0.7 broadcast_in_dim.38.phase_ref
  42.6 1.7 %first_phase.1 = (f32[128,128]{1,0:T(8,128)}, f32[64,128]{1,0:T(8,128)}) custom-call(s32[64,128]{1,0:T(8,128)} %broadcast_in_dim.38.phase_ref, f32[64,128]{1,0:T(8,128)S(1)} %get-tuple-element.199.live_ref, f32[64,128]{1,0:T(8,128)} %get-tuple-element.76.start_ref, f32[80,128]{1,0:T(8,128)S(1)} %get-tuple-element.198.here_ref, ...), custom_call_target="tpu_custom_call" | custom-call | tf_op jit(solution)/shard_map/first_phase/pallas_call | solution.py:362
  44.3 7.8 %collective-permute-start.7 = (f32[64,128]{1,0:T(8,128)}, f32[64,128]{1,0:T(8,128)S(1)}, u32[]{:S(2)}, u32[]{:S(2)}) collective-permute-start(f32[64,128]{1,0:T(8,128)} %get-tuple-element.77), channel_id=1, source_target_pairs={{1,2},{2,1},{3,4},{4,3},{5,6},{6,5},{7,8},{8,7},{9,10},{10,9},{11,... | collective-permute-start | bytes 98312 | tf_op jit(solution)/shard_map/ppermute | solution.py:297
  52.2 1.9 %collective-permute-done.7.delta_ref = f32[64,128]{1,0:T(8,128)S(1)} collective-permute-done((f32[64,128]{1,0:T(8,128)}, f32[64,128]{1,0:T(8,128)S(1)}, u32[]{:S(2)}, u32[]{:S(2)}) %collective-permute-start.7) | collective-permute-done | bytes 32800 | tf_op jit(solution)/shard_map/ppermute | solution.py:297
  54.0 0.6 copy-done.14
  54.7 1.5 %relay.2.mine_ref = f32[64,128]{1,0:T(8,128)} custom-call(f32[80,128]{1,0:T(8,128)S(1)} %get-tuple-element.198.here_ref, f32[64,128]{1,0:T(8,128)} %copy-done.14), custom_call_target="tpu_custom_call" | custom-call | tf_op jit(solution)/shard_map/relay/pallas_call | solution.py:369
  56.2 0.0 collective-permute-start.8
  56.2 0.2 fusion.3
  56.4 0.6 reduce_max.9
  57.7 1.4 %slice.12.beside_ref = f32[64,128]{1,0:T(8,128)} slice(f32[144,128]{1,0:T(8,128)} %copy-done.13), slice={[80:144], [0:128]} | slice | bytes 65536 | tf_op jit(solution)/shard_map/slice | solution.py:360
  59.0 0.0 collective-permute-done.8.other_ref
  59.0 0.6 copy-done.15
  59.7 1.2 %next_phase.2 = (f32[128,128]{1,0:T(8,128)S(1)}, f32[64,128]{1,0:T(8,128)S(1)}, f32[64,128]{1,0:T(8,128)S(1)}) custom-call(s32[1]{0:T(128)} %constant.9.clone.1.step_ref, s32[64,128]{1,0:T(8,128)} %broadcast_in_dim.38.phase_ref, f32[64,128]{1,0:T(8,128)S(1)} %get-tuple-element.199.live_ref, f32[80,128]{1,0:T(8,128)S(1)} %get-tuple-element.198.here_ref, ...), custom_call_target="tpu_custom_call" | custom-call | tf_op jit(solution)/shard_map/next_phase/pallas_call | solution.py:371
  60.9 7.8 %collective-permute-start.9 = (f32[64,128]{1,0:T(8,128)S(1)}, f32[64,128]{1,0:T(8,128)S(1)}, u32[]{:S(2)}, u32[]{:S(2)}) collective-permute-start(f32[64,128]{1,0:T(8,128)S(1)} %get-tuple-element.84), channel_id=1, source_target_pairs={{1,2},{2,1},{3,4},{4,3},{5,6},{6,5},{7,8},{8,7},{9,10},{10,9},{11,... | collective-permute-start | bytes 98312 | tf_op jit(solution)/shard_map/ppermute | solution.py:297
  68.6 1.7 %collective-permute-done.9.delta_ref = f32[64,128]{1,0:T(8,128)S(1)} collective-permute-done((f32[64,128]{1,0:T(8,128)S(1)}, f32[64,128]{1,0:T(8,128)S(1)}, u32[]{:S(2)}, u32[]{:S(2)}) %collective-permute-start.9) | collective-permute-done | bytes 32800 | tf_op jit(solution)/shard_map/ppermute | solution.py:297
  70.3 2.2 %copy-done.1 = bf16[64,64,512]{2,1,0:T(8,128)(2,1)S(1)} copy-done((bf16[64,64,512]{2,1,0:T(8,128)(2,1)S(1)}, bf16[64,64,512]{2,1,0:T(8,128)(2,1)}, u32[]{:S(2)}) %copy-start.1) | copy-done | bytes 4194328
  72.5 5.3 %spatial.1 = (f32[32,64]{1,0:T(8,128)}, bf16[32,32,128]{2,1,0:T(8,128)(2,1)S(1)}, bf16[32,32,128]{2,1,0:T(8,128)(2,1)S(1)}) custom-call(s32[1]{0:T(128)} %bitcast.core_ref, s32[4096]{0:T(1024)S(1)} %copy-done.5, bf16[64,64,512]{2,1,0:T(8,128)(2,1)S(1)} %copy-done.1, bf16[64,32,512]{2,1,0:T(8,128)(2,1)S(1)} %collective-permute-done.2.other_ref, ...), custom_call_target="tpu_custom_call" | custom-call | tf_op jit(solution)/shard_map/spatial/pallas_call | solution.py:380
  77.9 7.7 %collective-permute-start.10 = (bf16[32,32,128]{2,1,0:T(8,128)(2,1)S(1)}, bf16[32,32,128]{2,1,0:T(8,128)(2,1)S(1)}, u32[]{:S(2)}, u32[]{:S(2)}) collective-permute-start(bf16[32,32,128]{2,1,0:T(8,128)(2,1)S(1)} %get-tuple-element.87), channel_id=1, source_target_pairs={{1,2},{2,1},{3,4},{4,3},{5,6},{6,5},{7,8},{8,7},{9,10},{10,9},{11,... | collective-permute-start | bytes 786440 | tf_op jit(solution)/shard_map/ppermute | solution.py:297
  85.6 0.1 collective-permute-start.11
  85.7 4.0 %collective-permute-done.10.recv_ref = bf16[32,32,128]{2,1,0:T(8,128)(2,1)S(1)} collective-permute-done((bf16[32,32,128]{2,1,0:T(8,128)(2,1)S(1)}, bf16[32,32,128]{2,1,0:T(8,128)(2,1)S(1)}, u32[]{:S(2)}, u32[]{:S(2)}) %collective-permute-start.10) | collective-permute-done | bytes 262176 | tf_op jit(solution)/shard_map/ppermute | solution.py:297
  89.8 0.0 collective-permute-start.12
  89.8 1.5 %collective-permute-done.12.sib_recv_ref = bf16[32,32,128]{2,1,0:T(8,128)(2,1)S(1)} collective-permute-done((bf16[32,32,128]{2,1,0:T(8,128)(2,1)S(1)}, bf16[32,32,128]{2,1,0:T(8,128)(2,1)S(1)}, u32[]{:S(2)}, u32[]{:S(2)}) %collective-permute-start.12) | collective-permute-done | bytes 262176 | tf_op jit(solution)/shard_map/ppermute | solution.py:300
  91.3 0.7 copy-done.12
  92.0 2.8 %patches.1 = bf16[32,64,64]{2,1,0:T(8,128)(2,1)} custom-call(s32[32]{0:T(128)} %rows_ref.3, s32[32]{0:T(128)} %cols_ref.3, bf16[32,32,128]{2,1,0:T(8,128)(2,1)} %copy-done.3, bf16[32,32,128]{2,1,0:T(8,128)(2,1)} %copy-done.10, bf16[32,32,128]{2,1,0:T(8,128)(2,1)} %copy-done.11, bf16[32,32,128]{2,1,0:T(8,128)(2,1)} %copy-done.12), custom_call_target="tpu_custom_call" | custom-call | tf_op jit(solution)/shard_map/patches/pallas_call | solution.py:407
  (25 shorter events, 0.1 us)
Async XLA Ops:
  0.6 16.2 %copy-start.6 = (f32[32,64]{1,0:T(8,128)S(1)}, f32[32,64]{1,0:T(8,128)}, u32[]{:S(2)}) copy-start(f32[32,64]{1,0:T(8,128)} %near_ref.1) | copy-start | bytes 24580
  0.6 16.3 %copy-start.5 = (s32[4096]{0:T(1024)S(1)}, s32[4096]{0:T(1024)}, u32[]{:S(2)}) copy-start(s32[4096]{0:T(1024)} %colour_ref.3) | copy-start | bytes 49156
  0.7 20.4 %copy-start.7 = (s32[32]{0:T(128)S(1)}, s32[32]{0:T(128)}, u32[]{:S(2)}) copy-start(s32[32]{0:T(128)} %live_ref.3) | copy-start | bytes 388
  3.9 17.2 %collective-permute-start.2 = (bf16[64,32,512]{2,1,0:T(8,128)(2,1)}, bf16[64,32,512]{2,1,0:T(8,128)(2,1)S(1)}, u32[]{:S(2)}, u32[]{:S(2)}) collective-permute-start(bf16[64,32,512]{2,1,0:T(8,128)(2,1)} %constant_dynamic-slice_fusion), channel_id=1, source_target_pairs={{0,1},{1,0},{2,3},{3,2},{4,5},{5,4},{6,7},{7,6},{8,9},{9,8},{10,11... | collective-permute-start | bytes 6291464 | tf_op jit(solution)/shard_map/ppermute | solution.py:300
  6.2 14.8 %collective-permute-start.3 = (bf16[32,32,128]{2,1,0:T(8,128)(2,1)}, bf16[32,32,128]{2,1,0:T(8,128)(2,1)S(1)}, u32[]{:S(2)}, u32[]{:S(2)}) collective-permute-start(bf16[32,32,128]{2,1,0:T(8,128)(2,1)} %get-tuple-element.71), channel_id=1, source_target_pairs={{1,2},{2,1},{3,4},{4,3},{5,6},{6,5},{7,8},{8,7},{9,10},{10,9},{11,... | collective-permute-start | bytes 786440 | tf_op jit(solution)/shard_map/ppermute | solution.py:297
  16.8 1.3 %collective-permute-start.4 = (f32[32,64]{1,0:T(8,128)S(1)}, f32[32,64]{1,0:T(8,128)S(1)}, u32[]{:S(2)}, u32[]{:S(2)}) collective-permute-start(f32[32,64]{1,0:T(8,128)S(1)} %copy-done.6), channel_id=1, source_target_pairs={{0,1},{1,0},{2,3},{3,2},{4,5},{5,4},{6,7},{7,6},{8,9},{9,8},{10,11... | collective-permute-start | bytes 24584 | tf_op jit(solution)/shard_map/ppermute | solution.py:300
  21.1 2.2 %copy-start = (bf16[64,64,512]{2,1,0:T(8,128)(2,1)S(1)}, bf16[64,64,512]{2,1,0:T(8,128)(2,1)}, u32[]{:S(2)}) copy-start(bf16[64,64,512]{2,1,0:T(8,128)(2,1)} %mine_ref.3) | copy-start | bytes 12582916
  23.3 0.9 %copy-start.2 = (bf16[32,32,128]{2,1,0:T(8,128)(2,1)S(1)}, bf16[32,32,128]{2,1,0:T(8,128)(2,1)}, u32[]{:S(2)}) copy-start(bf16[32,32,128]{2,1,0:T(8,128)(2,1)} %get-tuple-element.70.own_ref) | copy-start | bytes 786436
  28.6 9.9 %copy-start.4 = (f32[144,128]{1,0:T(8,128)}, f32[144,128]{1,0:T(8,128)S(1)}, u32[]{:S(2)}) copy-start(f32[144,128]{1,0:T(8,128)S(1)} %get-tuple-element.74.mine_ref) | copy-start | bytes 221188
  28.6 9.9 %collective-permute-start.5 = (f32[144,128]{1,0:T(8,128)S(1)}, f32[144,128]{1,0:T(8,128)S(1)}, u32[]{:S(2)}, u32[]{:S(2)}) collective-permute-start(f32[144,128]{1,0:T(8,128)S(1)} %get-tuple-element.74.mine_ref), channel_id=1, source_target_pairs={{1,2},{2,1},{3,4},{4,3},{5,6},{6,5},{7,8},{8,7},{9,10},{10,9},{11,... | collective-permute-start | bytes 221192 | tf_op jit(solution)/shard_map/ppermute | solution.py:297
  38.5 0.6 copy-start.13
  40.7 1.2 %collective-permute-start.6 = (f32[80,128]{1,0:T(8,128)S(1)}, f32[80,128]{1,0:T(8,128)S(1)}, u32[]{:S(2)}, u32[]{:S(2)}) collective-permute-start(f32[80,128]{1,0:T(8,128)S(1)} %get-tuple-element.198.here_ref), channel_id=1, source_target_pairs={{0,1},{1,0},{2,3},{3,2},{4,5},{5,4},{6,7},{7,6},{8,9},{9,8},{10,11... | collective-permute-start | bytes 122888 | tf_op jit(solution)/shard_map/ppermute | solution.py:300
  44.3 9.7 %collective-permute-start.7 = (f32[64,128]{1,0:T(8,128)}, f32[64,128]{1,0:T(8,128)S(1)}, u32[]{:S(2)}, u32[]{:S(2)}) collective-permute-start(f32[64,128]{1,0:T(8,128)} %get-tuple-element.77), channel_id=1, source_target_pairs={{1,2},{2,1},{3,4},{4,3},{5,6},{6,5},{7,8},{8,7},{9,10},{10,9},{11,... | collective-permute-start | bytes 98312 | tf_op jit(solution)/shard_map/ppermute | solution.py:297
  54.0 0.6 copy-start.14
  56.2 2.9 %collective-permute-start.8 = (f32[64,128]{1,0:T(8,128)}, f32[64,128]{1,0:T(8,128)S(1)}, u32[]{:S(2)}, u32[]{:S(2)}) collective-permute-start(f32[64,128]{1,0:T(8,128)} %relay.2.mine_ref), channel_id=1, source_target_pairs={{0,1},{1,0},{2,3},{3,2},{4,5},{5,4},{6,7},{7,6},{8,9},{9,8},{10,11... | collective-permute-start | bytes 98312 | tf_op jit(solution)/shard_map/ppermute | solution.py:300
  59.0 0.6 copy-start.15
  60.9 9.5 %collective-permute-start.9 = (f32[64,128]{1,0:T(8,128)S(1)}, f32[64,128]{1,0:T(8,128)S(1)}, u32[]{:S(2)}, u32[]{:S(2)}) collective-permute-start(f32[64,128]{1,0:T(8,128)S(1)} %get-tuple-element.84), channel_id=1, source_target_pairs={{1,2},{2,1},{3,4},{4,3},{5,6},{6,5},{7,8},{8,7},{9,10},{10,9},{11,... | collective-permute-start | bytes 98312 | tf_op jit(solution)/shard_map/ppermute | solution.py:297
  70.3 2.2 %copy-start.1 = (bf16[64,64,512]{2,1,0:T(8,128)(2,1)S(1)}, bf16[64,64,512]{2,1,0:T(8,128)(2,1)}, u32[]{:S(2)}) copy-start(bf16[64,64,512]{2,1,0:T(8,128)(2,1)} %mine_ref.3) | copy-start | bytes 12582916
  77.9 13.4 %copy-start.3 = (bf16[32,32,128]{2,1,0:T(8,128)(2,1)}, bf16[32,32,128]{2,1,0:T(8,128)(2,1)S(1)}, u32[]{:S(2)}) copy-start(bf16[32,32,128]{2,1,0:T(8,128)(2,1)S(1)} %get-tuple-element.86.own_ref) | copy-start | bytes 786436
  77.9 11.9 %collective-permute-start.10 = (bf16[32,32,128]{2,1,0:T(8,128)(2,1)S(1)}, bf16[32,32,128]{2,1,0:T(8,128)(2,1)S(1)}, u32[]{:S(2)}, u32[]{:S(2)}) collective-permute-start(bf16[32,32,128]{2,1,0:T(8,128)(2,1)S(1)} %get-tuple-element.87), channel_id=1, source_target_pairs={{1,2},{2,1},{3,4},{4,3},{5,6},{6,5},{7,8},{8,7},{9,10},{10,9},{11,... | collective-permute-start | bytes 786440 | tf_op jit(solution)/shard_map/ppermute | solution.py:297
  85.6 4.2 %collective-permute-start.11 = (bf16[32,32,128]{2,1,0:T(8,128)(2,1)S(1)}, bf16[32,32,128]{2,1,0:T(8,128)(2,1)S(1)}, u32[]{:S(2)}, u32[]{:S(2)}) collective-permute-start(bf16[32,32,128]{2,1,0:T(8,128)(2,1)S(1)} %get-tuple-element.86.own_ref), channel_id=1, source_target_pairs={{0,1},{1,0},{2,3},{3,2},{4,5},{5,4},{6,7},{7,6},{8,9},{9,8},{10,11... | collective-permute-start | bytes 786440 | tf_op jit(solution)/shard_map/ppermute | solution.py:300
  89.8 1.5 %copy-start.10 = (bf16[32,32,128]{2,1,0:T(8,128)(2,1)}, bf16[32,32,128]{2,1,0:T(8,128)(2,1)S(1)}, u32[]{:S(2)}) copy-start(bf16[32,32,128]{2,1,0:T(8,128)(2,1)S(1)} %collective-permute-done.10.recv_ref) | copy-start | bytes 786436
  89.8 1.5 %collective-permute-start.12 = (bf16[32,32,128]{2,1,0:T(8,128)(2,1)S(1)}, bf16[32,32,128]{2,1,0:T(8,128)(2,1)S(1)}, u32[]{:S(2)}, u32[]{:S(2)}) collective-permute-start(bf16[32,32,128]{2,1,0:T(8,128)(2,1)S(1)} %collective-permute-done.10.recv_ref), channel_id=1, source_target_pairs={{0,1},{1,0},{2,3},{3,2},{4,5},{5,4},{6,7},{7,6},{8,9},{9,8},{10,11... | collective-permute-start | bytes 786440 | tf_op jit(solution)/shard_map/ppermute | solution.py:300
  89.8 1.5 %copy-start.11 = (bf16[32,32,128]{2,1,0:T(8,128)(2,1)}, bf16[32,32,128]{2,1,0:T(8,128)(2,1)S(1)}, u32[]{:S(2)}) copy-start(bf16[32,32,128]{2,1,0:T(8,128)(2,1)S(1)} %collective-permute-done.11.sib_own_ref) | copy-start | bytes 786436
  91.3 0.7 copy-start.12

commit v2 on v1

--- a/solution.py
+++ b/solution.py
@@ -47,8 +47,18 @@
     return jnp.where(other >= tiles, tile - 1, other)
 
 
-def slab_kernel(rows_ref, cols_ref, live_ref, patches_ref, out_ref, own_ref):
+def slab_kernel(
+    rows_ref, cols_ref, live_ref, patches_ref, movie_ref, out_ref, own_ref, keep_ref, send_ref, sems,
+):
     core = lax.axis_index("frame")
+    sends = pltpu.make_async_copy(
+        movie_ref.at[:, pl.ds(pl.multiple_of(HALF * (1 - core), HALF), HALF), :], send_ref, sems.at[0]
+    )
+    keeps = pltpu.make_async_copy(
+        movie_ref.at[:, pl.ds(pl.multiple_of(HALF * core, HALF), HALF), :], keep_ref, sems.at[1]
+    )
+    sends.start()
+    keeps.start()
     line = iota((PATCH, PATCH), 0)
     base_out = jnp.where(core == 0, 0, 96)
     base_own = jnp.where(core == 0, 32, 64)
@@ -63,17 +73,44 @@
         spread = dot(placed, col_pick).astype(bf16)
         out_ref[s] = spread[:HALF]
         own_ref[s] = spread[HALF:]
+    sends.wait()
+    keeps.wait()
+
+
+def table_kernel(
+    colour_ref, live_ref, traces_ref, phase_ref, live_rows_ref, begin_ref, count_ref, owner_ref
+):
+    tile = lax.axis_index("tile")
+    live_rows_ref[...] = jnp.zeros_like(live_rows_ref)
+    for i in range(GROUP):
+        owner_ref[i] = 0
+    for s in range(SLOTS):
+        at = (s // LAYERS) * COLOURS + colour_ref[tile * SLOTS + s]
+        owner_ref[at] = 1
+        alive = live_ref[s].astype(f32)
+        live_rows_ref[pl.ds(at, 1), :] = jnp.full((1, FRAMES), alive, f32)
+        begin_ref[s : s + 1, :] = traces_ref[s : s + 1, :] * alive
+    most = jnp.int32(0)
+    for b in range(BINS):
+        phase = jnp.int32(0)
+        for g in range(COLOURS):
+            i = b * COLOURS + g
+            if g:
+                phase = phase + jnp.abs(owner_ref[i] - owner_ref[i - 1])
+            value = jnp.where(owner_ref[i] == 1, phase, -1)
+            phase_ref[i : i + 1, :] = jnp.full((1, FRAMES), value, jnp.int32)
+        most = jnp.maximum(most, phase + 1)
+    count_ref[0] = most
 
 
 def partial_kernel(
-    tiles, core_ref, colour_ref, live_ref, mine_ref, other_ref, own_ref, recv_ref,
-    near_ref, far_ref, slab_ref, message_ref, live_rows_ref,
+    tiles, colour_ref, mine_ref, other_ref, own_ref, recv_ref, near_ref, far_ref,
+    slab_ref, message_ref,
 ):
     tile = lax.axis_index("tile")
     core = lax.axis_index("frame")
     beside = neighbour_tile(tile, core, tiles)
     message_ref[...] = jnp.zeros_like(message_ref)
-    live_rows_ref[...] = jnp.zeros_like(live_rows_ref)
     start = GROUP + COLOURS
     wide = jnp.concatenate([near_ref[...], far_ref[...]], axis=1)
     swapped = jnp.concatenate([far_ref[...], near_ref[...]], axis=1)
@@ -84,9 +121,7 @@
         theirs = b * COLOURS + colour_ref[beside * SLOTS + s]
         slab_ref[mine] = own_ref[s]
         slab_ref[theirs] = recv_ref[s]
-        alive = live_ref[s].astype(f32)
-        message_ref[pl.ds(start + mine, 1), :] = first[s : s + 1] * alive
-        live_rows_ref[pl.ds(mine, 1), :] = jnp.full((1, FRAMES), alive, f32)
+        message_ref[pl.ds(start + mine, 1), :] = first[s : s + 1]
     same_row = iota((1024, 256), 0) % 16 == iota((1024, 256), 1) % 16
     fold = jnp.where(iota((COLOURS, 256), 1) // 16 == iota((COLOURS, 256), 0), 1.0, 0.0)
     gram = jnp.zeros((COLOURS, EDGE), f32)
@@ -120,17 +155,6 @@
     return jnp.where(keep, tall, 0.0)
 
 
-def join_kernel(mine_ref, pair_ref, out_ref, start_ref):
-    grams = slice(GROUP, GROUP + COLOURS)
-    traces = slice(GROUP + COLOURS, 2 * GROUP + COLOURS)
-    gram = mine_ref[grams, :] + pair_ref[grams, :]
-    current = mine_ref[traces, :] + pair_ref[traces, :]
-    drive = mine_ref[:GROUP, :] + pair_ref[:GROUP, :]
-    out_ref[:GROUP, :] = drive - dot(block_diagonal(gram), current, exact)
-    out_ref[grams, :] = gram
-    start_ref[...] = mine_ref[traces, :]
-
-
 def settle(phase_ref, live_ref, gram, residual, current, phase, state_ref, change_ref):
     whole = jnp.concatenate([gram] * BINS, axis=0)
     lane = iota((GROUP, EDGE), 1)
@@ -158,34 +182,48 @@
         change_ref[rows, :] = change
 
 
-def first_phase_kernel(phase_ref, live_ref, start_ref, here_ref, there_ref, state_ref, change_ref):
+def first_phase_kernel(
+    phase_ref, live_ref, mine_ref, pair_ref, far_ref, far_pair_ref,
+    state_ref, change_ref, gram_ref, beside_ref,
+):
+    drives = slice(0, GROUP)
     grams = slice(GROUP, GROUP + COLOURS)
-    gram = here_ref[grams, :] + there_ref[grams, :]
-    residual = here_ref[:GROUP, :] + there_ref[:GROUP, :]
-    settle(phase_ref, live_ref, gram, residual, start_ref[...], 0, state_ref, change_ref)
-
-
-def relay_kernel(here_ref, delta_ref, out_ref):
-    grams = slice(GROUP, GROUP + COLOURS)
-    out_ref[...] = dot(block_diagonal(here_ref[grams, :]), delta_ref[...], exact)
+    traces = slice(GROUP + COLOURS, 2 * GROUP + COLOURS)
+    here = mine_ref[grams, :] + pair_ref[grams, :]
+    there = far_ref[grams, :] + far_pair_ref[grams, :]
+    drive = mine_ref[drives, :] + pair_ref[drives, :] + far_ref[drives, :] + far_pair_ref[drives, :]
+    start = mine_ref[traces, :]
+    coupled = dot(block_diagonal(here + there), start, exact)
+    coupled = coupled + dot(block_diagonal(here), pair_ref[traces, :], exact)
+    coupled = coupled + dot(block_diagonal(there), far_pair_ref[traces, :], exact)
+    gram_ref[:COLOURS, :] = here
+    gram_ref[COLOURS:, :] = there
+    beside_ref[...] = pair_ref[traces, :]
+    settle(phase_ref, live_ref, here + there, drive - coupled, start, 0, state_ref, change_ref)
 
 
 def next_phase_kernel(
-    step_ref, phase_ref, live_ref, here_ref, there_ref, mine_ref, other_ref, old_ref, beside_ref,
-    delta_ref, state_ref, change_ref, beside_out_ref,
-):
-    grams = slice(GROUP, GROUP + COLOURS)
-    gram = here_ref[grams, :] + there_ref[grams, :]
-    residual = old_ref[:GROUP, :] - (mine_ref[...] + other_ref[...])
-    current = old_ref[GROUP:, :]
+    step_ref, phase_ref, live_ref, gram_ref, old_ref, beside_ref, delta_ref, far_delta_ref,
+    state_ref, change_ref, beside_out_ref,
+):
+    here = gram_ref[:COLOURS, :]
+    there = gram_ref[COLOURS:, :]
+    coupled = dot(block_diagonal(here), delta_ref[...], exact)
+    coupled = coupled + dot(block_diagonal(there), far_delta_ref[...], exact)
+    residual = old_ref[:GROUP, :] - coupled
     beside_out_ref[...] = beside_ref[...] + delta_ref[...]
-    settle(phase_ref, live_ref, gram, residual, current, step_ref[0], state_ref, change_ref)
+    settle(
+        phase_ref, live_ref, here + there, residual, old_ref[GROUP:, :], step_ref[0],
+        state_ref, change_ref,
+    )
 
 
 def spatial_kernel(
-    tiles, core_ref, colour_ref, mine_ref, other_ref, slab_ref, state_in_ref, beside_ref, delta_ref,
-    traces_ref, out_ref, own_ref, weight_ref, cross_ref, field_ref, state_ref,
-):
+    tiles, colour_ref, mine_ref, other_ref, slab_ref, state_in_ref, beside_ref, delta_ref,
+    traces_ref, out_ref, own_ref, weight_ref, cross_ref, field_ref, state_ref, far_ref, sem,
+):
+    fetch = pltpu.make_async_copy(other_ref, far_ref, sem)
+    fetch.start()
     tile = lax.axis_index("tile")
     core = lax.axis_index("frame")
     beside = neighbour_tile(tile, core, tiles)
@@ -201,6 +239,7 @@
     repeat = jnp.where(position == iota((FRAMES, 2048), 0), 1.0, 0.0).astype(bf16)
     repeated = dot(both.astype(bf16), repeat)
     same_row = iota((16, 2048), 0) == iota((16, 2048), 1) % 16
+    fetch.wait()
     for b in range(BINS):
         rows = slice(b * COLOURS, (b + 1) * COLOURS)
         lanes = slice(b * EDGE, (b + 1) * EDGE)
@@ -208,7 +247,7 @@
             line = repeated[b * COLOURS + g : b * COLOURS + g + 1]
             weight_ref[16 * g : 16 * g + 16, :] = jnp.where(same_row, line, 0.0).astype(bf16)
         pixels = []
-        for ref in (mine_ref, other_ref):
+        for ref in (mine_ref, far_ref):
             part = [ref[:, 16 * q : 16 * q + 16, lanes].reshape(1024, EDGE) for q in range(2)]
             pixels.append(jnp.concatenate(part, axis=1))
         field_ref[b] = dot(weight_ref[...], jnp.concatenate(pixels, axis=0))
@@ -273,22 +312,20 @@
     return jax.ShapeDtypeStruct(dims, dtype)
 
 
-def call(kernel, ins, outs, name, scratch=(), limit=None):
+def call(kernel, ins, outs, name, limit, scratch=(), out_specs=None):
     return pl.pallas_call(
         kernel,
         in_specs=ins,
-        out_specs=[vmem] * len(outs),
+        out_specs=out_specs or [vmem] * len(outs),
         out_shape=outs,
         scratch_shapes=list(scratch),
         name=name,
-        compiler_params=pltpu.CompilerParams(vmem_limit_bytes=limit) if limit else None,
+        compiler_params=pltpu.CompilerParams(vmem_limit_bytes=limit * 2**20),
     )
 
 
 def on_device(movie_block, patches, patch_rows, patch_cols, neuron_live, neuron_colour, traces):
     tiles = lax.axis_size("tile")
-    core = lax.axis_index("frame")
-    tile = lax.axis_index("tile")
     swap_pairs = []
     for t in range(tiles - 1):
         swap_pairs += [(2 * t + 1, 2 * t + 2), (2 * t + 2, 2 * t + 1)]
@@ -299,113 +336,98 @@
     def chip_swap(value):
         return lax.ppermute(value, "frame", [(0, 1), (1, 0)])
 
-    own_colour = lax.dynamic_slice_in_dim(neuron_colour, tile * SLOTS, SLOTS)
-    owned = jnp.any(
-        own_colour.reshape(BINS, LAYERS, 1) == jnp.arange(COLOURS, dtype=jnp.int32), axis=1
-    )
-    turns = (owned[:, 1:] != owned[:, :-1]).astype(jnp.int32)
-    later = jnp.arange(COLOURS)[None, :] > jnp.arange(COLOURS - 1)[:, None]
-    phase_of = jnp.sum(jnp.where(later[None], turns[:, :, None], 0), axis=1)
-    phase_count = jnp.max(jnp.sum(turns, axis=1)) + 1
-    phases = jnp.where(owned, phase_of, -1).reshape(GROUP, 1)
-    phases = jnp.broadcast_to(phases, (GROUP, FRAMES))
-
-    movie_out = lax.dynamic_slice_in_dim(movie_block, HALF * (1 - core), HALF, 1)
+    piece = shape((SLOTS, HALF, EDGE), bf16)
+    strip = shape((64, HALF, 512), bf16)
+    group = shape((GROUP, FRAMES))
+    hbm = pl.BlockSpec(memory_space=pltpu.HBM)
+    movie_block = pltpu.with_memory_space_constraint(movie_block, pltpu.HBM)
+    piece_out, piece_own, movie_mine, movie_out = call(
+        slab_kernel,
+        [smem, smem, smem, vmem, hbm],
+        [piece, piece, strip, strip],
+        "slabs",
+        12,
+        [pltpu.SemaphoreType.DMA((2,))],
+    )(patch_rows, patch_cols, neuron_live, patches, movie_block)
     movie_other = chip_swap(movie_out)
-    traces_other = chip_swap(traces)
-
-    piece_out, piece_own = call(
-        slab_kernel,
-        [smem, smem, smem, vmem],
-        [shape((SLOTS, HALF, EDGE), bf16)] * 2,
-        "slabs",
-    )(patch_rows, patch_cols, neuron_live, patches)
+    movie_kept = pltpu.with_memory_space_constraint(movie_other, pltpu.HBM)
     piece_recv = pair_swap(piece_out)
-
-    core_at = core.reshape(1)
-    movie_spec = pl.BlockSpec((64, HALF, 512), lambda i, c: (0, c[0], 0))
-    whole2 = lambda dims: pl.BlockSpec(dims, lambda i, c: (0,) * len(dims))
-    smem_in = pl.BlockSpec(memory_space=pltpu.SMEM)
-
-    slab, message, live_rows = pl.pallas_call(
+    phases, live_rows, begin, phase_count = call(
+        table_kernel,
+        [smem, smem, vmem],
+        [
+            shape((GROUP, FRAMES), jnp.int32), group, shape((SLOTS, 64)), shape((1,), jnp.int32)
+        ],
+        "tables",
+        2,
+        [pltpu.SMEM((GROUP,), jnp.int32)],
+        [vmem, vmem, vmem, smem],
+    )(neuron_colour, neuron_live, traces)
+    begin_far = chip_swap(begin)
+
+    slab, message = call(
         functools.partial(partial_kernel, tiles),
-        grid_spec=pltpu.PrefetchScalarGridSpec(
-            num_scalar_prefetch=1,
-            grid=(1,),
-            in_specs=[
-                smem_in, smem_in, movie_spec, whole2((64, HALF, 512)), whole2((SLOTS, HALF, EDGE)),
-                whole2((SLOTS, HALF, EDGE)), whole2((SLOTS, 64)), whole2((SLOTS, 64)),
-            ],
-            out_specs=[
-                whole2((GROUP, HALF, EDGE)), whole2((2 * GROUP + COLOURS, FRAMES)),
-                whole2((GROUP, FRAMES)),
-            ],
-        ),
-        out_shape=[
-            shape((GROUP, HALF, EDGE), bf16), shape((2 * GROUP + COLOURS, FRAMES)),
-            shape((GROUP, FRAMES)),
-        ],
-        compiler_params=pltpu.CompilerParams(vmem_limit_bytes=40 * 2**20),
-        name="partial_sums",
+        [smem] + [vmem] * 6,
+        [shape((GROUP, HALF, EDGE), bf16), shape((2 * GROUP + COLOURS, FRAMES))],
+        "partial_sums",
+        20,
     )(
-        core_at, neuron_colour, neuron_live, movie_block, movie_other, piece_own, piece_recv,
-        traces, traces_other,
-    )
-
+        neuron_colour, movie_mine, movie_other, piece_own, piece_recv, begin, begin_far
+    )
+
+    message_far = chip_swap(message)
     message_pair = pair_swap(message)
-    here, start = call(
-        join_kernel, [vmem] * 2, [shape((GROUP + COLOURS, FRAMES)), shape((GROUP, FRAMES))], "join"
-    )(message, message_pair)
-    there = chip_swap(here)
-    beside = message_pair[GROUP + COLOURS :]
-    state_shapes = [shape((2 * GROUP, FRAMES)), shape((GROUP, FRAMES))]
-    state, change = call(first_phase_kernel, [vmem] * 5, state_shapes, "first_phase")(
-        phases, live_rows, start, here, there
-    )
+    message_far_pair = chip_swap(message_pair)
+    state, change, gram, beside = call(
+        first_phase_kernel,
+        [vmem] * 6,
+        [shape((2 * GROUP, FRAMES)), group, shape((2 * COLOURS, FRAMES)), group],
+        "first_phase",
+        4,
+    )(phases, live_rows, message, message_pair, message_far, message_far_pair)
 
     def advance(carry):
         step, state, beside, change = carry
         delta = pair_swap(change)
-        (mine,) = call(relay_kernel, [vmem] * 2, [shape((GROUP, FRAMES))], "relay")(here, delta)
-        other = chip_swap(mine)
+        far_delta = chip_swap(delta)
         state, change, beside = call(
-            next_phase_kernel, [smem] + [vmem] * 9, state_shapes + [shape((GROUP, FRAMES))], "next_phase"
-        )(step.reshape(1), phases, live_rows, here, there, mine, other, state, beside, delta)
+            next_phase_kernel,
+            [smem] + [vmem] * 7,
+            [shape((2 * GROUP, FRAMES)), group, group],
+            "next_phase",
+            4,
+        )(step.reshape(1), phases, live_rows, gram, state, beside, delta, far_delta)
         return step + 1, state, beside, change
 
     carry = advance((jnp.int32(1), state, beside, change))
-    _, state, beside, change = lax.while_loop(lambda c: c[0] < phase_count, advance, carry)
+    _, state, beside, change = lax.while_loop(lambda c: c[0] < phase_count[0], advance, carry)
     delta = pair_swap(change)
 
-    new_traces, final_out, final_own = pl.pallas_call(
+    new_traces, final_out, final_own = call(
         functools.partial(spatial_kernel, tiles),
-        grid_spec=pltpu.PrefetchScalarGridSpec(
-            num_scalar_prefetch=1,
-            grid=(1,),
-            in_specs=[
-                smem_in, movie_spec, whole2((64, HALF, 512)), whole2((GROUP, HALF, EDGE)),
-                whole2((2 * GROUP, FRAMES)), whole2((GROUP, FRAMES)), whole2((GROUP, FRAMES)),
-            ],
-            out_specs=[whole2((SLOTS, 64)), whole2((SLOTS, HALF, EDGE)), whole2((SLOTS, HALF, EDGE))],
-            scratch_shapes=[
-                pltpu.VMEM((256, 2048), bf16),
-                pltpu.VMEM((GROUP * COLOURS, EDGE), f32),
-                pltpu.VMEM((BINS, 256, 256), f32),
-                pltpu.VMEM((GROUP, HALF, EDGE), bf16),
-            ],
-        ),
-        out_shape=[
-            shape((SLOTS, 64)), shape((SLOTS, HALF, EDGE), bf16), shape((SLOTS, HALF, EDGE), bf16)
+        [smem, vmem, hbm] + [vmem] * 4,
+        [shape((SLOTS, 64)), piece, piece],
+        "spatial",
+        20,
+        [
+            pltpu.VMEM((256, 2048), bf16),
+            pltpu.VMEM((GROUP * COLOURS, EDGE), f32),
+            pltpu.VMEM((BINS, 256, 256), f32),
+            pltpu.VMEM((GROUP, HALF, EDGE), bf16),
+            pltpu.VMEM((64, HALF, 512), bf16),
+            pltpu.SemaphoreType.DMA(()),
         ],
-        compiler_params=pltpu.CompilerParams(vmem_limit_bytes=40 * 2**20),
-        name="spatial",
-    )(core_at, neuron_colour, movie_block, movie_other, slab, state, beside, delta)
+    )(neuron_colour, movie_mine, movie_kept, slab, state, beside, delta)
 
     far_own = chip_swap(final_own)
     final_recv = pair_swap(final_out)
     far_recv = chip_swap(final_recv)
     (new_patches,) = call(
-        patch_kernel, [smem, smem] + [vmem] * 4, [shape((SLOTS, PATCH, PATCH), bf16)], "patches"
+        patch_kernel,
+        [smem, smem] + [vmem] * 4,
+        [shape((SLOTS, PATCH, PATCH), bf16)],
+        "patches",
+        8,
     )(patch_rows, patch_cols, final_own, final_recv, far_own, far_recv)
     return (new_traces, new_patches)
 

time: 95.8 us -> 81.8 us (0.85)
  local copies, waits for them, and re-layouts: 13.5 us -> 3.02 us
  Pallas kernels: 20.8 us -> 19 us
  other arithmetic: 1.09 us -> 0 us
    unnamed x28 -> x18, local copies, waits for them, and re-layouts: 7.89 us -> 3.02 us
    dynamic_slice x2 -> x0, local copies, waits for them, and re-layouts: 3.27 us -> none  [the longest x1 3.2 us: on_device(): lax.dynamic_slice_in_dim(movie_block, HALF * (1 - core), HALF, 1)]
    ppermute x5, waiting for transfers between devices: 12.5 us -> 10.2 us  [pair_swap(): return lax.ppermute(value, ('tile', 'frame'), swap_pairs)]
    ppermute x6 -> x7, waiting for transfers between devices: 3.37 us -> 5.17 us  [chip_swap(): return lax.ppermute(value, 'frame', [(0, 1), (1, 0)])]
    slice x1 -> x0, local copies, waits for them, and re-layouts: 1.38 us -> none  [on_device(): beside = message_pair[GROUP + COLOURS:]]
    pallas_call x7 -> x6, Pallas kernels: 18.1 us -> 16.8 us  [the longest x1 7.02 us: on_device(): call(functools.partial(spatial_kernel, tiles), [smem, vmem, hbm] + [vmem]...]
  transfers between devices with their start and end apart: 11 -> 12, of which waited for: 8 -> 9; matrix products, arithmetic and copies ran while one was open for 3% -> 0% of each run, Pallas kernels for 2% -> 2%
where the time goes in v2:
time: 81.8 us; the launch traced here: 81.2 us
  starting transfers between devices  42.4 us (52%)
  Pallas kernels  19 us (23%)
  waiting for transfers between devices  15.4 us (19%)
  local copies, waits for them, and re-layouts  3.02 us (4%)
    ppermute x5, starting transfers between devices, pair_swap(): return lax.ppermute(value, ('tile', 'frame'), swap_pairs)  42 us
    ppermute x5, waiting for transfers between devices, pair_swap(): return lax.ppermute(value, ('tile', 'frame'), swap_pairs)  10.2 us
    pallas_call x1, Pallas kernels, on_device(): call(functools.partial(spatial_kernel, tiles), [smem, vmem, hbm] + [vmem]...  7.02 us
    ppermute x7, waiting for transfers between devices, chip_swap(): return lax.ppermute(value, 'frame', [(0, 1), (1, 0)])  5.17 us
    pallas_call x1, Pallas kernels, on_device(): call(functools.partial(partial_kernel, tiles), [smem] + [vmem] * 6, [shap...  4.36 us
    pallas_call x1, Pallas kernels, on_device(): call(slab_kernel, [smem, smem, smem, vmem, hbm], [piece, piece, strip, st...  3.16 us
    unnamed x18, local copies, waits for them, and re-layouts  3.02 us
    pallas_call x1, Pallas kernels, on_device(): call(patch_kernel, [smem, smem] + [vmem] * 4, [shape((SLOTS, PATCH, PATCH...  2.12 us
  transfers between devices with their start and end apart: 12, of which 9 were waited for; matrix products, arithmetic and copies ran while one was open for 0% of the time, Pallas kernels for 2%

profile of v2, /device:TPU:6, one launch (start us, length us, event | category | flops | bytes accessed | tf_op | source)
XLA Modules:
  0.0 81.2 jit_solution(3732601381526851882)
XLA Ops:
  0.6 0.0 copy-start.1
  0.6 1.0 %copy-done.1 = bf16[32,64,64]{2,1,0:T(8,128)(2,1)S(1)} copy-done((bf16[32,64,64]{2,1,0:T(8,128)(2,1)S(1)}, bf16[32,64,64]{2,1,0:T(8,128)(2,1)}, u32[]{:S(2)}) %copy-start.1) | copy-done | bytes 262168
  1.7 0.0 copy-start.4
  1.7 0.7 copy-done.4
  2.3 0.0 copy-start.5
  2.3 0.7 copy-done.5
  3.0 0.0 copy-start.7
  3.0 0.7 copy-done.7
  3.6 0.0 copy-start.2
  3.6 0.0 copy-start.3
  3.6 3.2 %slabs.1 = (bf16[32,32,128]{2,1,0:T(8,128)(2,1)S(1)}, bf16[32,32,128]{2,1,0:T(8,128)(2,1)S(1)}, bf16[64,32,512]{2,1,0:T(8,128)(2,1)S(1)}, bf16[64,32,512]{2,1,0:T(8,128)(2,1)S(1)}) custom-call(s32[32]{0:T(128)S(1)} %copy-done.5, s32[32]{0:T(128)S(1)} %copy-done.7, s32[32]{0:T(128)S(1)} %copy-done.4, bf16[32,64,64]{2,1,0:T(8,128)(2,1)S(1)} %copy-done.1, ...), custom_call_target="tpu_custom_call" | custom-call | tf_op jit(solution)/shard_map/slabs/pallas_call | solution.py:344
  6.8 0.1 collective-permute-start.2
  6.9 10.6 %collective-permute-start.3 = (bf16[32,32,128]{2,1,0:T(8,128)(2,1)S(1)}, bf16[32,32,128]{2,1,0:T(8,128)(2,1)S(1)}, u32[]{:S(2)}, u32[]{:S(2)}) collective-permute-start(bf16[32,32,128]{2,1,0:T(8,128)(2,1)S(1)} %get-tuple-element.73), channel_id=1, source_target_pairs={{1,2},{2,1},{3,4},{4,3},{5,6},{6,5},{7,8},{8,7},{9,10},{10,9},{11,... | collective-permute-start | bytes 786440 | tf_op jit(solution)/shard_map/ppermute | solution.py:334
  17.5 0.0 copy-done.2
  17.5 0.0 copy-done.3
  17.5 1.6 %tables.1 = (s32[64,128]{1,0:T(8,128)S(1)}, f32[64,128]{1,0:T(8,128)S(1)}, f32[32,64]{1,0:T(8,128)S(1)}, s32[1]{0:T(128)}) custom-call(s32[4096]{0:T(1024)S(1)} %copy-done.2, s32[32]{0:T(128)S(1)} %copy-done.4, f32[32,64]{1,0:T(8,128)S(1)} %copy-done.3), custom_call_target="tpu_custom_call" | custom-call | tf_op jit(solution)/shard_map/tables/pallas_call | solution.py:355
  19.1 0.1 collective-permute-start.4
  19.2 1.2 %collective-permute-done.4.far_ref = f32[32,64]{1,0:T(8,128)S(1)} collective-permute-done((f32[32,64]{1,0:T(8,128)S(1)}, f32[32,64]{1,0:T(8,128)S(1)}, u32[]{:S(2)}, u32[]{:S(2)}) %collective-permute-start.4) | collective-permute-done | bytes 8224 | tf_op jit(solution)/shard_map/ppermute | solution.py:337
  20.4 1.2 %collective-permute-done.3.recv_ref = bf16[32,32,128]{2,1,0:T(8,128)(2,1)S(1)} collective-permute-done((bf16[32,32,128]{2,1,0:T(8,128)(2,1)S(1)}, bf16[32,32,128]{2,1,0:T(8,128)(2,1)S(1)}, u32[]{:S(2)}, u32[]{:S(2)}) %collective-permute-start.3) | collective-permute-done | bytes 262176 | tf_op jit(solution)/shard_map/ppermute | solution.py:334
  21.5 0.0 collective-permute-done.2.other_ref
  21.5 0.0 copy-start
  21.5 4.4 %partial_sums.1 = (bf16[64,32,128]{2,1,0:T(8,128)(2,1)S(1)}, f32[144,128]{1,0:T(8,128)S(1)}) custom-call(s32[4096]{0:T(1024)S(1)} %copy-done.2, bf16[64,32,512]{2,1,0:T(8,128)(2,1)S(1)} %get-tuple-element.70.mine_ref, bf16[64,32,512]{2,1,0:T(8,128)(2,1)S(1)} %collective-permute-done.2.other_ref, bf16[32,32,128]{2,1,0:T(8,128)(2,1)S(1)} %get-tuple-element.72.own_ref, ...), custom_call_target="tpu_custom_call" | custom-call | tf_op jit(solution)/shard_map/partial_sums/pallas_call | solution.py:368
  25.9 0.0 copy-done
  25.9 7.9 %collective-permute-start.5 = (f32[144,128]{1,0:T(8,128)S(1)}, f32[144,128]{1,0:T(8,128)S(1)}, u32[]{:S(2)}, u32[]{:S(2)}) collective-permute-start(f32[144,128]{1,0:T(8,128)S(1)} %get-tuple-element.78.mine_ref), channel_id=1, source_target_pairs={{1,2},{2,1},{3,4},{4,3},{5,6},{6,5},{7,8},{8,7},{9,10},{10,9},{11,... | collective-permute-start | bytes 221192 | tf_op jit(solution)/shard_map/ppermute | solution.py:334
  33.8 0.1 collective-permute-start.6
  33.9 1.9 %collective-permute-done.5.pair_ref = f32[144,128]{1,0:T(8,128)S(1)} collective-permute-done((f32[144,128]{1,0:T(8,128)S(1)}, f32[144,128]{1,0:T(8,128)S(1)}, u32[]{:S(2)}, u32[]{:S(2)}) %collective-permute-start.5) | collective-permute-done | bytes 73760 | tf_op jit(solution)/shard_map/ppermute | solution.py:334
  35.8 0.0 collective-permute-start.7
  35.8 0.0 collective-permute-done.6.far_ref
  35.8 1.3 %collective-permute-done.7.far_pair_ref = f32[144,128]{1,0:T(8,128)S(1)} collective-permute-done((f32[144,128]{1,0:T(8,128)S(1)}, f32[144,128]{1,0:T(8,128)S(1)}, u32[]{:S(2)}, u32[]{:S(2)}) %collective-permute-start.7) | collective-permute-done | bytes 73760 | tf_op jit(solution)/shard_map/ppermute | solution.py:337
  37.1 0.4 first_phase.1
  37.5 7.9 %collective-permute-start.8 = (f32[64,128]{1,0:T(8,128)S(1)}, f32[64,128]{1,0:T(8,128)S(1)}, u32[]{:S(2)}, u32[]{:S(2)}) collective-permute-start(f32[64,128]{1,0:T(8,128)S(1)} %get-tuple-element.82), channel_id=1, source_target_pairs={{1,2},{2,1},{3,4},{4,3},{5,6},{6,5},{7,8},{8,7},{9,10},{10,9},{11,... | collective-permute-start | bytes 98312 | tf_op jit(solution)/shard_map/ppermute | solution.py:334
  45.3 1.6 %collective-permute-done.8.delta_ref = f32[64,128]{1,0:T(8,128)S(1)} collective-permute-done((f32[64,128]{1,0:T(8,128)S(1)}, f32[64,128]{1,0:T(8,128)S(1)}, u32[]{:S(2)}, u32[]{:S(2)}) %collective-permute-start.8) | collective-permute-done | bytes 32800 | tf_op jit(solution)/shard_map/ppermute | solution.py:334
  46.9 0.0 collective-permute-start.9
  46.9 1.2 %collective-permute-done.9.far_delta_ref = f32[64,128]{1,0:T(8,128)S(1)} collective-permute-done((f32[64,128]{1,0:T(8,128)S(1)}, f32[64,128]{1,0:T(8,128)S(1)}, u32[]{:S(2)}, u32[]{:S(2)}) %collective-permute-start.9) | collective-permute-done | bytes 32800 | tf_op jit(solution)/shard_map/ppermute | solution.py:337
  48.1 0.4 next_phase.2
  48.5 0.7 while.14
  49.1 7.9 %collective-permute-start.10 = (f32[64,128]{1,0:T(8,128)S(1)}, f32[64,128]{1,0:T(8,128)S(1)}, u32[]{:S(2)}, u32[]{:S(2)}) collective-permute-start(f32[64,128]{1,0:T(8,128)S(1)} %get-tuple-element.89), channel_id=1, source_target_pairs={{1,2},{2,1},{3,4},{4,3},{5,6},{6,5},{7,8},{8,7},{9,10},{10,9},{11,... | collective-permute-start | bytes 98312 | tf_op jit(solution)/shard_map/ppermute | solution.py:334
  57.0 1.6 %collective-permute-done.10.delta_ref = f32[64,128]{1,0:T(8,128)S(1)} collective-permute-done((f32[64,128]{1,0:T(8,128)S(1)}, f32[64,128]{1,0:T(8,128)S(1)}, u32[]{:S(2)}, u32[]{:S(2)}) %collective-permute-start.10) | collective-permute-done | bytes 32800 | tf_op jit(solution)/shard_map/ppermute | solution.py:334
  58.6 7.0 %spatial.1 = (f32[32,64]{1,0:T(8,128)}, bf16[32,32,128]{2,1,0:T(8,128)(2,1)S(1)}, bf16[32,32,128]{2,1,0:T(8,128)(2,1)S(1)}) custom-call(s32[4096]{0:T(1024)S(1)} %copy-done.2, bf16[64,32,512]{2,1,0:T(8,128)(2,1)S(1)} %get-tuple-element.70.mine_ref, bf16[64,32,512]{2,1,0:T(8,128)(2,1)} %copy-done, bf16[64,32,128]{2,1,0:T(8,128)(2,1)S(1)} %get-tuple-element.75.slab_ref, ...), custom_call_target="tpu_custom_call" | custom-call | tf_op jit(solution)/shard_map/spatial/pallas_call | solution.py:406
  65.6 7.9 %collective-permute-start.11 = (bf16[32,32,128]{2,1,0:T(8,128)(2,1)S(1)}, bf16[32,32,128]{2,1,0:T(8,128)(2,1)S(1)}, u32[]{:S(2)}, u32[]{:S(2)}) collective-permute-start(bf16[32,32,128]{2,1,0:T(8,128)(2,1)S(1)} %get-tuple-element.92), channel_id=1, source_target_pairs={{1,2},{2,1},{3,4},{4,3},{5,6},{6,5},{7,8},{8,7},{9,10},{10,9},{11,... | collective-permute-start | bytes 786440 | tf_op jit(solution)/shard_map/ppermute | solution.py:334
  73.5 0.1 collective-permute-start.12
  73.6 3.9 %collective-permute-done.11.recv_ref = bf16[32,32,128]{2,1,0:T(8,128)(2,1)S(1)} collective-permute-done((bf16[32,32,128]{2,1,0:T(8,128)(2,1)S(1)}, bf16[32,32,128]{2,1,0:T(8,128)(2,1)S(1)}, u32[]{:S(2)}, u32[]{:S(2)}) %collective-permute-start.11) | collective-permute-done | bytes 262176 | tf_op jit(solution)/shard_map/ppermute | solution.py:334
  77.5 0.0 collective-permute-start.13
  77.5 0.0 collective-permute-done.12.sib_own_ref
  77.5 1.5 %collective-permute-done.13.sib_recv_ref = bf16[32,32,128]{2,1,0:T(8,128)(2,1)S(1)} collective-permute-done((bf16[32,32,128]{2,1,0:T(8,128)(2,1)S(1)}, bf16[32,32,128]{2,1,0:T(8,128)(2,1)S(1)}, u32[]{:S(2)}, u32[]{:S(2)}) %collective-permute-start.13) | collective-permute-done | bytes 262176 | tf_op jit(solution)/shard_map/ppermute | solution.py:337
  79.1 0.0 copy-done.6
  79.1 0.0 copy-done.8
  79.1 2.1 %patches.1 = bf16[32,64,64]{2,1,0:T(8,128)(2,1)} custom-call(s32[32]{0:T(128)S(1)} %copy-done.6, s32[32]{0:T(128)S(1)} %copy-done.8, bf16[32,32,128]{2,1,0:T(8,128)(2,1)S(1)} %get-tuple-element.91.own_ref, bf16[32,32,128]{2,1,0:T(8,128)(2,1)S(1)} %collective-permute-done.11.recv_ref, bf16[32,32,128]{2,1,0:T(8,128)(2,1)S(1)} %collective-permute-done.12.sib_own_ref, ...), custom_call_target="tpu_custom_call" | custom-call | tf_op jit(solution)/shard_map/patches/pallas_call | solution.py:425
  (2 shorter events, 0.0 us)
Async XLA Ops:
  0.6 1.0 %copy-start.1 = (bf16[32,64,64]{2,1,0:T(8,128)(2,1)S(1)}, bf16[32,64,64]{2,1,0:T(8,128)(2,1)}, u32[]{:S(2)}) copy-start(bf16[32,64,64]{2,1,0:T(8,128)(2,1)} %patches_ref.1) | copy-start | bytes 786436
  1.7 0.7 copy-start.4
  2.3 0.7 copy-start.5
  3.0 0.7 copy-start.7
  3.6 13.9 %copy-start.2 = (s32[4096]{0:T(1024)S(1)}, s32[4096]{0:T(1024)}, u32[]{:S(2)}) copy-start(s32[4096]{0:T(1024)} %colour_ref.5) | copy-start | bytes 49156
  3.6 13.9 %copy-start.3 = (f32[32,64]{1,0:T(8,128)S(1)}, f32[32,64]{1,0:T(8,128)}, u32[]{:S(2)}) copy-start(f32[32,64]{1,0:T(8,128)} %traces_ref.1) | copy-start | bytes 24580
  6.8 14.7 %collective-permute-start.2 = (bf16[64,32,512]{2,1,0:T(8,128)(2,1)S(1)}, bf16[64,32,512]{2,1,0:T(8,128)(2,1)S(1)}, u32[]{:S(2)}, u32[]{:S(2)}) collective-permute-start(bf16[64,32,512]{2,1,0:T(8,128)(2,1)S(1)} %get-tuple-element.71), channel_id=1, source_target_pairs={{0,1},{1,0},{2,3},{3,2},{4,5},{5,4},{6,7},{7,6},{8,9},{9,8},{10,11... | collective-permute-start | bytes 6291464 | tf_op jit(solution)/shard_map/ppermute | solution.py:337
  6.9 14.6 %collective-permute-start.3 = (bf16[32,32,128]{2,1,0:T(8,128)(2,1)S(1)}, bf16[32,32,128]{2,1,0:T(8,128)(2,1)S(1)}, u32[]{:S(2)}, u32[]{:S(2)}) collective-permute-start(bf16[32,32,128]{2,1,0:T(8,128)(2,1)S(1)} %get-tuple-element.73), channel_id=1, source_target_pairs={{1,2},{2,1},{3,4},{4,3},{5,6},{6,5},{7,8},{8,7},{9,10},{10,9},{11,... | collective-permute-start | bytes 786440 | tf_op jit(solution)/shard_map/ppermute | solution.py:334
  19.1 1.3 %collective-permute-start.4 = (f32[32,64]{1,0:T(8,128)S(1)}, f32[32,64]{1,0:T(8,128)S(1)}, u32[]{:S(2)}, u32[]{:S(2)}) collective-permute-start(f32[32,64]{1,0:T(8,128)S(1)} %get-tuple-element.74.near_ref), channel_id=1, source_target_pairs={{0,1},{1,0},{2,3},{3,2},{4,5},{5,4},{6,7},{7,6},{8,9},{9,8},{10,11... | collective-permute-start | bytes 24584 | tf_op jit(solution)/shard_map/ppermute | solution.py:337
  21.5 4.4 %copy-start = (bf16[64,32,512]{2,1,0:T(8,128)(2,1)}, bf16[64,32,512]{2,1,0:T(8,128)(2,1)S(1)}, u32[]{:S(2)}) copy-start(bf16[64,32,512]{2,1,0:T(8,128)(2,1)S(1)} %collective-permute-done.2.other_ref) | copy-start | bytes 6291460
  25.9 9.9 %collective-permute-start.5 = (f32[144,128]{1,0:T(8,128)S(1)}, f32[144,128]{1,0:T(8,128)S(1)}, u32[]{:S(2)}, u32[]{:S(2)}) collective-permute-start(f32[144,128]{1,0:T(8,128)S(1)} %get-tuple-element.78.mine_ref), channel_id=1, source_target_pairs={{1,2},{2,1},{3,4},{4,3},{5,6},{6,5},{7,8},{8,7},{9,10},{10,9},{11,... | collective-permute-start | bytes 221192 | tf_op jit(solution)/shard_map/ppermute | solution.py:334
  33.8 2.0 %collective-permute-start.6 = (f32[144,128]{1,0:T(8,128)S(1)}, f32[144,128]{1,0:T(8,128)S(1)}, u32[]{:S(2)}, u32[]{:S(2)}) collective-permute-start(f32[144,128]{1,0:T(8,128)S(1)} %get-tuple-element.78.mine_ref), channel_id=1, source_target_pairs={{0,1},{1,0},{2,3},{3,2},{4,5},{5,4},{6,7},{7,6},{8,9},{9,8},{10,11... | collective-permute-start | bytes 221192 | tf_op jit(solution)/shard_map/ppermute | solution.py:337
  35.8 1.3 %collective-permute-start.7 = (f32[144,128]{1,0:T(8,128)S(1)}, f32[144,128]{1,0:T(8,128)S(1)}, u32[]{:S(2)}, u32[]{:S(2)}) collective-permute-start(f32[144,128]{1,0:T(8,128)S(1)} %collective-permute-done.5.pair_ref), channel_id=1, source_target_pairs={{0,1},{1,0},{2,3},{3,2},{4,5},{5,4},{6,7},{7,6},{8,9},{9,8},{10,11... | collective-permute-start | bytes 221192 | tf_op jit(solution)/shard_map/ppermute | solution.py:337
  37.5 9.5 %collective-permute-start.8 = (f32[64,128]{1,0:T(8,128)S(1)}, f32[64,128]{1,0:T(8,128)S(1)}, u32[]{:S(2)}, u32[]{:S(2)}) collective-permute-start(f32[64,128]{1,0:T(8,128)S(1)} %get-tuple-element.82), channel_id=1, source_target_pairs={{1,2},{2,1},{3,4},{4,3},{5,6},{6,5},{7,8},{8,7},{9,10},{10,9},{11,... | collective-permute-start | bytes 98312 | tf_op jit(solution)/shard_map/ppermute | solution.py:334
  46.9 1.2 %collective-permute-start.9 = (f32[64,128]{1,0:T(8,128)S(1)}, f32[64,128]{1,0:T(8,128)S(1)}, u32[]{:S(2)}, u32[]{:S(2)}) collective-permute-start(f32[64,128]{1,0:T(8,128)S(1)} %collective-permute-done.8.delta_ref), channel_id=1, source_target_pairs={{0,1},{1,0},{2,3},{3,2},{4,5},{5,4},{6,7},{7,6},{8,9},{9,8},{10,11... | collective-permute-start | bytes 98312 | tf_op jit(solution)/shard_map/ppermute | solution.py:337
  49.1 9.5 %collective-permute-start.10 = (f32[64,128]{1,0:T(8,128)S(1)}, f32[64,128]{1,0:T(8,128)S(1)}, u32[]{:S(2)}, u32[]{:S(2)}) collective-permute-start(f32[64,128]{1,0:T(8,128)S(1)} %get-tuple-element.89), channel_id=1, source_target_pairs={{1,2},{2,1},{3,4},{4,3},{5,6},{6,5},{7,8},{8,7},{9,10},{10,9},{11,... | collective-permute-start | bytes 98312 | tf_op jit(solution)/shard_map/ppermute | solution.py:334
  58.6 20.5 %copy-start.6 = (s32[32]{0:T(128)S(1)}, s32[32]{0:T(128)}, u32[]{:S(2)}) copy-start(s32[32]{0:T(128)} %rows_ref.3) | copy-start | bytes 388
  58.6 20.5 %copy-start.8 = (s32[32]{0:T(128)S(1)}, s32[32]{0:T(128)}, u32[]{:S(2)}) copy-start(s32[32]{0:T(128)} %cols_ref.3) | copy-start | bytes 388
  65.6 11.9 %collective-permute-start.11 = (bf16[32,32,128]{2,1,0:T(8,128)(2,1)S(1)}, bf16[32,32,128]{2,1,0:T(8,128)(2,1)S(1)}, u32[]{:S(2)}, u32[]{:S(2)}) collective-permute-start(bf16[32,32,128]{2,1,0:T(8,128)(2,1)S(1)} %get-tuple-element.92), channel_id=1, source_target_pairs={{1,2},{2,1},{3,4},{4,3},{5,6},{6,5},{7,8},{8,7},{9,10},{10,9},{11,... | collective-permute-start | bytes 786440 | tf_op jit(solution)/shard_map/ppermute | solution.py:334
  73.5 4.0 %collective-permute-start.12 = (bf16[32,32,128]{2,1,0:T(8,128)(2,1)S(1)}, bf16[32,32,128]{2,1,0:T(8,128)(2,1)S(1)}, u32[]{:S(2)}, u32[]{:S(2)}) collective-permute-start(bf16[32,32,128]{2,1,0:T(8,128)(2,1)S(1)} %get-tuple-element.91.own_ref), channel_id=1, source_target_pairs={{0,1},{1,0},{2,3},{3,2},{4,5},{5,4},{6,7},{7,6},{8,9},{9,8},{10,11... | collective-permute-start | bytes 786440 | tf_op jit(solution)/shard_map/ppermute | solution.py:337
  77.5 1.5 %collective-permute-start.13 = (bf16[32,32,128]{2,1,0:T(8,128)(2,1)S(1)}, bf16[32,32,128]{2,1,0:T(8,128)(2,1)S(1)}, u32[]{:S(2)}, u32[]{:S(2)}) collective-permute-start(bf16[32,32,128]{2,1,0:T(8,128)(2,1)S(1)} %collective-permute-done.11.recv_ref), channel_id=1, source_target_pairs={{0,1},{1,0},{2,3},{3,2},{4,5},{5,4},{6,7},{7,6},{8,9},{9,8},{10,11... | collective-permute-start | bytes 786440 | tf_op jit(solution)/shard_map/ppermute | solution.py:337
